TPU v7x, 32 devices: a whole 2x2x4 slice. The times are simulated.
32 devices in a mesh: stream: 16 (over z, y, x), cross: 2 (over core).
Axes of the slice: x: 2, y: 2, z: 4, core: 2. Of those that a mesh axis runs over, the one named last changes fastest.
Arguments:
- source: float32 [128, 16, 128], P('stream', 'cross'), may hold values from -6 to 6
- metric: float32 [16, 2, 16], P('stream', 'cross'), may hold values from 0.5 to 4
- base_velocity: float32 [3, 128, 16, 128], P(None, 'stream', 'cross'), may hold values from -6 to 6
- drop_elem: int32 [16, 2, 5, 128], P('stream', 'cross'), may hold values from 0 to 511, as said below
- drop_coord: float32 [16, 2, 5, 3, 128], P('stream', 'cross'), may hold values from -1 to 1
- drop_vel: float32 [16, 2, 5, 3, 128], P('stream', 'cross'), may hold values from -6 to 6
- drop_prop: float32 [16, 2, 5, 2, 128], P('stream', 'cross'), may hold values from 0.5 to 4
- drop_counts: int32 [16, 2, 5], P('stream', 'cross'), may hold values from 0 to 128, as said below
Outputs:
- pressure: float32 [128, 16, 128], P('stream', 'cross')
- momentum_source: float32 [3, 128, 16, 128], P(None, 'stream', 'cross')
- drop_accel: float32 [16, 2, 5, 3, 128], P('stream', 'cross')
Inputs may be any that keep to these rules, and one draw needn't show every extreme that they name: `drop_elem`: elements are numbered (ex * 2 + ey) * 16 + ez. The owner element of every slot of block b of holder (s, c) lies in slab s + b - 2 (streamwise element index from (s + b - 2) * 1 to that plus 1 - 1) and column c (element index from c * 1 to c + 1 - 1); this holds for slots that are not live as well, for blocks whose slab lies in the grid. `drop_counts`: A block whose owner slab s + b - 2 lies outside 0 to 15 has count 0. In every draw some slab of some column receives 128 live droplets from each of its 5 holder slabs.
All inputs are finite; a program needn't handle non-finite values.
Results may differ from a plain program's by a relative error of at most 0.0003.
Values sent between devices are 32-bit elements; how exact they have to be, the bound alone decides.
No kernel may reach another device: no remote copies, remote signals or barrier semaphores. Data moves between devices by JAX's collectives and lax.ppermute only.
A program may use at most 64 MiB of HBM per device.

v0:
```python
import jax
import jax.numpy as jnp
import numpy as np
from jax import lax
from jax.experimental import pallas as pl
from jax.experimental.pallas import tpu as pltpu
from jax.sharding import PartitionSpec as P


SWEEPS = 3
DEPTH = SWEEPS + 1
NODES = 8
MASS_SHIFT = 1.0
UPPER_BOUND = 2.5
LOWER_BOUND = UPPER_BOUND / 30.0
GLL_POINTS = [
    -1.0,
    -0.8717401485096066,
    -0.5917001814331423,
    -0.2092992179024789,
    0.2092992179024789,
    0.5917001814331423,
    0.8717401485096066,
    1.0,
]
F32 = jnp.float32
BF16 = jnp.bfloat16
ROUTES = ((1, 0), (1, 1), (2, 0), (2, 1))


def legendre_seven(points):
    before = points * 0.0 + 1.0
    current = points
    for order in range(1, 7):
        following = ((2.0 * order + 1.0) * points * current - order * before) / (order + 1.0)
        before = current
        current = following
    return current


def gll_tables():
    gll_nodes = np.array(GLL_POINTS)
    values = legendre_seven(gll_nodes)
    weights = 2.0 / (56.0 * values * values)
    deriv_mat = np.zeros((8, 8))
    for row_idx in range(8):
        for col_idx in range(8):
            if row_idx != col_idx:
                deriv_mat[row_idx, col_idx] = values[row_idx] / (
                    values[col_idx] * (gll_nodes[row_idx] - gll_nodes[col_idx])
                )
    deriv_mat[0, 0] = -14.0
    deriv_mat[7, 7] = 14.0
    return (gll_nodes, weights, deriv_mat)


NODE_POS, WEIGHTS, DERIV = gll_tables()
STIFF = DERIV.T @ (WEIGHTS[:, None] * DERIV)
STIFF_DIAG = np.diag(STIFF)


def split_pair(table):
    high = table.astype(np.float32).astype(jnp.bfloat16)
    low = (table - high.astype(np.float64)).astype(np.float32).astype(jnp.bfloat16)
    return high, low


def lane_weights(matrix, lanes):
    full = np.kron(np.eye(lanes // NODES), matrix.T)
    high, low = split_pair(full)
    zero = np.zeros_like(np.asarray(low))
    return np.concatenate(
        [np.concatenate([high, low], 1), np.concatenate([high, zero], 1)], 0
    ).astype(jnp.bfloat16)


T_KY, T_DY = 0, 8
T_WJ, T_QJ, T_WK, T_QK, T_Z7, T_Z0, T_Y7, T_Y0 = range(16, 24)
T_NODE = 24
T_INV = 31
T_COUNT = 32


def table_tiles(lanes):
    tiles = np.zeros((T_COUNT, NODES, lanes))
    for turn in range(NODES):
        for row in range(NODES):
            tiles[T_KY + turn, row, :] = STIFF[row, (row - turn) % NODES]
            tiles[T_DY + turn, row, :] = DERIV[row, (row - turn) % NODES]
    reps = lanes // NODES
    tiles[T_WJ] = WEIGHTS[:, None]
    tiles[T_QJ] = STIFF_DIAG[:, None]
    tiles[T_WK] = np.tile(WEIGHTS, reps)[None, :]
    tiles[T_QK] = np.tile(STIFF_DIAG, reps)[None, :]
    place = np.arange(lanes)
    tiles[T_Z7] = ((place % NODES == NODES - 1) & (place < lanes - 1))[None, :]
    tiles[T_Z0] = ((place % NODES == 0) & (place > 0))[None, :]
    tiles[T_Y7, NODES - 1] = 1.0
    tiles[T_Y0, 0] = 1.0
    for row in range(NODES):
        others = [m for m in range(NODES) if m != row]
        scale = 1.0
        for slot, other in enumerate(others):
            tiles[T_NODE + slot, row, :] = NODE_POS[other]
            scale *= NODE_POS[row] - NODE_POS[other]
        tiles[T_INV, row, :] = 1.0 / scale
    return tiles.astype(np.float32)


def bit_pairs(count, bit):
    return [(i, i ^ bit) for i in range(count)]


def neighbour_pairs(count, distance, odd):
    pairs = []
    for low in range(count - distance):
        if (low // distance) % 2 == odd:
            pairs += [(low, low + distance), (low + distance, low)]
    return pairs


def route_block(position, route, reach):
    distance, odd = route
    upward = (position // distance) % 2 == odd
    middle = (reach - 1) // 2
    return jnp.where(upward, middle + distance, middle - distance)


def split_value(value):
    high = value.astype(BF16)
    low = (value - high.astype(F32)).astype(BF16)
    return high, low


def pack_kernel(cols, reach, spread_ref, source, metric, elem, coord, vel, prop, counts, *outs):
    packed, own, routed = outs[0], outs[1], outs[2:6]
    state = outs[6]
    position = lax.axis_index("stream")
    column = lax.axis_index("cross")
    elem_z = metric.shape[-1]
    packed[0:NODES] = source[...]
    row = jnp.broadcast_to(metric[0, 0][None, :], (NODES, elem_z))
    packed[NODES] = jnp.dot(row, spread_ref[...], precision=lax.Precision.HIGHEST, preferred_element_type=F32)
    capacity = elem.shape[-1]
    middle = (reach - 1) // 2
    slot = lax.broadcasted_iota(jnp.int32, (1, capacity), 1)
    for block in range(reach):
        base = ((position + (block - middle)) * cols + column) * elem_z
        local = elem[block] - base + 1
        live = slot < counts[0, 0, block]
        ids = jnp.where(live, local, 0).astype(F32)
        for axis in range(3):
            state[block, axis : axis + 1, :] = coord[3 * block + axis]
            state[block, 3 + axis : 4 + axis, :] = vel[3 * block + axis]
        state[block, 6:8, :] = prop[0, 0, block]
        state[block, 8:16, :] = jnp.broadcast_to(ids, (8, capacity))
    own[...] = state[middle]
    for route, out in zip(ROUTES, routed):
        out[...] = state[route_block(position, route, reach)]


def z_assembled(block, tiles):
    lanes = block.shape[-1]
    axis = block.ndim - 1
    after = pltpu.roll(block, lanes - 1, axis)
    before = pltpu.roll(block, 1, axis)
    return block + tiles[T_Z7] * after + tiles[T_Z0] * before


def y_assembled(blocks, tiles):
    axis = blocks[0].ndim - 2
    out = []
    for j, block in enumerate(blocks):
        total = block
        if j + 1 < len(blocks):
            total = total + tiles[T_Y7] * pltpu.roll(blocks[j + 1], NODES - 1, axis)
        if j > 0:
            total = total + tiles[T_Y0] * pltpu.roll(blocks[j - 1], 1, axis)
        out.append(total)
    return out


def x_product(planes, matrix):
    out = []
    for row in range(NODES):
        total = None
        for col in range(NODES):
            term = planes[col] * float(matrix[row, col])
            total = term if total is None else total + term
        out.append(total)
    return out


def y_product(block, tiles, start):
    total = block * tiles[start]
    for turn in range(1, NODES):
        total = total + pltpu.roll(block, turn, block.ndim - 2) * tiles[start + turn]
    return total


def z_product(rows, weights):
    lanes = rows.shape[-1]
    high, low = split_value(rows)
    both = jnp.concatenate([high, low], axis=1)
    wide = jnp.dot(both, weights, preferred_element_type=F32)
    return wide[:, :lanes] + wide[:, lanes:]


def lagrange(row, tiles):
    capacity = row.shape[-1]
    coords = jnp.broadcast_to(row, (NODES, capacity))
    factor = tiles[T_INV]
    for slot in range(NODES - 1):
        factor = factor * (coords - tiles[T_NODE + slot])
    return factor


def main_kernel(slabs, cols, *refs):
    tiles, stiff_w, deriv_w = refs[0:3]
    pieces = refs[3 : 3 + 3 * cols]
    base_velocity, own = refs[3 + 3 * cols : 5 + 3 * cols]
    routed = refs[5 + 3 * cols : 9 + 3 * cols]
    (pressure, momentum, face_even, face_odd, acc_own, acc_e1, acc_o1, acc_e2, acc_o2,
     loads, scales, resid, update, inv, work, zed) = refs[9 + 3 * cols :]
    lanes = tiles.shape[-1]
    position = lax.axis_index("stream")
    column = lax.axis_index("cross")
    span = 2 * DEPTH - 1
    middle = DEPTH - 1

    group_even = (position // DEPTH) % 2 == 0
    rank = position % DEPTH
    wjk = tiles[T_WJ] * tiles[T_WK]
    for slot_c in range(cols):
        col = column ^ slot_c
        for kind in range(3):
            if kind == 0:
                shift = 0
            elif kind == 1:
                shift = jnp.where(group_even, DEPTH, -DEPTH)
            else:
                shift = jnp.where(group_even, -DEPTH, DEPTH)
            piece = pieces[3 * slot_c + kind]
            for slot in range(DEPTH):
                at = (rank ^ slot) - rank + shift + (2 * DEPTH - 1)
                for i in range(NODES):
                    loads[at, col, i] = piece[slot, i] * (wjk * float(WEIGHTS[i]))
                scales[at, col] = piece[slot, NODES]
    wide_mid = 2 * DEPTH - 1

    def present(offset):
        where = position + offset
        return jnp.where((where >= 0) & (where < slabs), 1.0, 0.0).astype(F32)

    def sides(offset):
        at = wide_mid + offset
        stacks, diags = [], []
        for j in range(cols):
            stacks.append(z_assembled(loads[at, j], tiles))
        stacks = y_assembled(stacks, tiles)
        pres = present(offset)
        for j in range(cols):
            scale = scales[at, j]
            alpha = z_assembled(scale * tiles[T_WK], tiles)
            beta = z_assembled(scale * tiles[T_QK] + (MASS_SHIFT * pres) * tiles[T_WK], tiles)
            rows = []
            for i in range(NODES):
                first = tiles[T_WJ] * float(STIFF_DIAG[i]) + tiles[T_QJ] * float(WEIGHTS[i])
                rows.append(alpha * first + beta * (tiles[T_WJ] * float(WEIGHTS[i])))
            diags.append(jnp.stack(rows, 0))
        diags = y_assembled(diags, tiles)
        return stacks, diags

    def sides_body(step, carry):
        offset = step - DEPTH
        stacks, diags = sides(offset)
        for j in range(cols):
            work[step, j] = stacks[j]
            zed[step, j] = diags[j]
        return carry

    lax.fori_loop(0, 2 * DEPTH + 1, sides_body, 0)

    center = (UPPER_BOUND + LOWER_BOUND) / 2.0
    half_width = (UPPER_BOUND - LOWER_BOUND) / 2.0
    ratio_bound = center / half_width
    cheb_rho = 1.0 / ratio_bound

    def start_body(step, carry):
        gap = 1.0 - present(step - middle)
        for j in range(cols):
            for i in range(NODES):
                side = work[step + 1, j, i]
                diag = zed[step + 1, j, i]
                if i == 0:
                    side = side + work[step, j, NODES - 1]
                    diag = diag + zed[step, j, NODES - 1]
                if i == NODES - 1:
                    side = side + work[step + 2, j, 0]
                    diag = diag + zed[step + 2, j, 0]
                inverse = 1.0 / (diag + gap)
                inv[step, j, i] = inverse
                resid[step, j, i] = side
                update[step, j, i] = side * inverse * (1.0 / center)
        return carry

    lax.fori_loop(0, span, start_body, 0)

    iterate = update[middle, column]
    for sweep in range(SWEEPS):
        radius = SWEEPS - sweep
        first = middle - radius
        count = 2 * radius + 1
        rows = update[first : first + count].reshape(count * cols * NODES * NODES, lanes)
        zed[0:count] = z_product(rows, stiff_w[...]).reshape(count, cols, NODES, NODES, lanes)

        def operator_body(step, carry, first=first):
            offset = step + first - middle
            pres = present(offset)
            outs = []
            for j in range(cols):
                scale = scales[wide_mid + offset, j]
                scaled = scale * tiles[T_WK]
                value = update[first + step, j]
                planes = [value[i] for i in range(NODES)]
                from_x = x_product(planes, STIFF)
                mass = (MASS_SHIFT * pres) * wjk
                scale_x = scaled * tiles[T_WJ]
                scale_z = scale * tiles[T_WJ]
                local = []
                for i in range(NODES):
                    weight = float(WEIGHTS[i])
                    from_y = y_product(planes[i], tiles, T_KY)
                    rest = scaled * from_y + scale_z * zed[step, j, i] + mass * planes[i]
                    local.append(scale_x * from_x[i] + rest * weight)
                outs.append(z_assembled(jnp.stack(local, 0), tiles))
            outs = y_assembled(outs, tiles)
            for j in range(cols):
                work[step, j] = outs[j]
            return carry

        lax.fori_loop(0, count, operator_body, 0)
        rho_next = 1.0 / (2.0 * ratio_bound - cheb_rho)

        def update_body(step, carry, first=first, rho_next=rho_next, cheb_rho=cheb_rho):
            at = first + 1 + step
            for j in range(cols):
                for i in range(NODES):
                    total = work[step + 1, j, i]
                    if i == 0:
                        total = total + work[step, j, NODES - 1]
                    if i == NODES - 1:
                        total = total + work[step + 2, j, 0]
                    left = resid[at, j, i] - total
                    resid[at, j, i] = left
                    update[at, j, i] = (rho_next * cheb_rho) * update[at, j, i] + (
                        2.0 * rho_next / half_width
                    ) * (inv[at, j, i] * left)
            return carry

        lax.fori_loop(0, count - 2, update_body, 0)
        cheb_rho = rho_next
        iterate = iterate + update[middle, column]
    pressure[...] = iterate

    scale = scales[wide_mid, column]
    planes = [iterate[i] for i in range(NODES)]
    grad_x = x_product(planes, DERIV)
    grad_z = z_product(iterate.reshape(NODES * NODES, lanes), deriv_w[...]).reshape(NODES, NODES, lanes)
    velocity = []
    for i in range(NODES):
        velocity.append(base_velocity[0, i] - scale * grad_x[i])
    for i in range(NODES):
        velocity.append(base_velocity[1, i] - scale * y_product(planes[i], tiles, T_DY))
    for i in range(NODES):
        velocity.append(base_velocity[2, i] - scale * grad_z[i])
    velocity = jnp.concatenate(velocity, 0)

    groups = (own,) + tuple(routed)
    pick, bases = [], []
    for group in groups:
        basis = [lagrange(group[axis : axis + 1, :], tiles) for axis in range(3)]
        ids = group[8:16, :]
        pick.append(jnp.concatenate(
            [jnp.where(ids == float(e + 1), basis[2], 0.0) for e in range(lanes // NODES)], 0))
        bases.append(basis)
    pick = jnp.concatenate(pick, 1)
    pick_high, pick_low = split_value(pick)
    vel_high, vel_low = split_value(velocity)
    partial = jnp.dot(
        jnp.concatenate([vel_high, vel_low, vel_high], 1),
        jnp.concatenate([pick_high, pick_high, pick_low], 0),
        preferred_element_type=F32,
    )
    capacity = own.shape[-1]
    spread = []
    for g, (group, basis) in enumerate(zip(groups, bases)):
        ids = group[8:9, :]
        cells = [basis[1] * basis[0][i : i + 1, :] for i in range(NODES)]
        accel_rows, parts = [], []
        for comp in range(3):
            total = None
            for i in range(NODES):
                row = (comp * NODES + i) * NODES
                term = partial[row : row + NODES, g * capacity : (g + 1) * capacity] * cells[i]
                total = term if total is None else total + term
            fluid = jnp.sum(total, axis=0, keepdims=True)
            accel = jnp.where(ids > 0.5, group[6:7, :] * (fluid - group[3 + comp : 4 + comp, :]), 0.0)
            accel_rows.append(accel)
            force = -group[7:8, :] * accel
            parts += [cells[i] * force for i in range(NODES)]
        accel_rows.append(jnp.zeros((NODES - 3, capacity), F32))
        (acc_own, acc_e1, acc_o1, acc_e2, acc_o2)[g][...] = jnp.concatenate(accel_rows, 0)
        spread.append(jnp.concatenate(parts, 0))
    spread = jnp.concatenate(spread, 1)
    spread_high, spread_low = split_value(spread)
    added = lax.dot_general(
        jnp.concatenate([spread_high, spread_low, spread_high], 1),
        jnp.concatenate([pick_high, pick_high, pick_low], 1),
        (((1,), (1,)), ((), ())),
        preferred_element_type=F32,
    )
    added = z_assembled(added.reshape(3, NODES, NODES, lanes), tiles)
    momentum[...] = added
    low_row = added[:, :, 0, :]
    high_row = added[:, :, NODES - 1, :]
    even = column % 2 == 0
    face_even[...] = jnp.where(even, high_row, low_row)
    face_odd[...] = jnp.where(even, low_row, high_row)


def middle_kernel(cols, momentum, face_even, face_odd, acc_e1, acc_o1, out, send_e1, send_o1):
    position = lax.axis_index("stream")
    column = lax.axis_index("cross")
    even = column % 2 == 0
    high = jnp.where(even, face_even[...], face_odd[...]) if cols > 2 else jnp.where(even, face_even[...], 0.0)
    low = jnp.where(even, face_odd[...], face_even[...]) if cols > 2 else jnp.where(even, 0.0, face_even[...])
    out[...] = momentum[...]
    out[:, :, 0, :] = momentum[:, :, 0, :] + low
    out[:, :, NODES - 1, :] = momentum[:, :, NODES - 1, :] + high
    lower = position % 2 == 0
    top = jnp.where(lower, NODES - 1, 0)
    bottom = NODES - 1 - top
    for comp in range(3):
        send_e1[comp] = out[comp, top]
        send_o1[comp] = out[comp, bottom]
    send_e1[3] = acc_e1[...]
    send_o1[3] = acc_o1[...]


def last_kernel(reach, momentum, got_e1, got_o1, acc_own, got_e2, got_o2, out, accel):
    position = lax.axis_index("stream")
    lower = position % 2 == 0
    top = jnp.where(lower, NODES - 1, 0)
    bottom = NODES - 1 - top
    out[...] = momentum[...]
    for comp in range(3):
        out[comp, top] = momentum[comp, top] + got_e1[comp]
        out[comp, bottom] = momentum[comp, bottom] + got_o1[comp]
    for axis in range(3):
        accel[3 * ((reach - 1) // 2) + axis] = acc_own[axis : axis + 1]
    arrived = (got_e1[3], got_o1[3], got_e2[...], got_o2[...])
    for route, value in zip(ROUTES, arrived):
        block = route_block(position, route, reach)
        for axis in range(3):
            accel[3 * block + axis] = value[axis : axis + 1]


def f32(*shape):
    return jax.ShapeDtypeStruct(shape, F32)


def near(*shape):
    return pltpu.VMEM(shape, F32)


def held(value):
    return pltpu.with_memory_space_constraint(value, pltpu.VMEM)


def step(
    source, metric, base_velocity, drop_elem, drop_coord, drop_vel, drop_prop, drop_counts
):
    slabs = lax.axis_size("stream")
    cols = lax.axis_size("cross")
    lanes = source.shape[-1]
    reach, capacity = drop_elem.shape[2:]
    elem_z = metric.shape[-1]
    vmem = pl.BlockSpec(memory_space=pltpu.VMEM)
    smem = pl.BlockSpec(memory_space=pltpu.SMEM)
    tiles = jnp.asarray(table_tiles(lanes))
    stiff_w = jnp.asarray(lane_weights(STIFF, lanes))
    deriv_w = jnp.asarray(lane_weights(DERIV, lanes))
    to_lanes = jnp.asarray(np.kron(np.eye(elem_z), np.ones((1, NODES))), F32)

    packed, own, *routed = pl.pallas_call(
        lambda *refs: pack_kernel(cols, reach, *refs),
        out_shape=[near(NODES + 1, NODES, lanes)] + [near(16, capacity)] * 5,
        in_specs=[vmem] * 7 + [smem],
        out_specs=[vmem] * 6,
        scratch_shapes=[pltpu.VMEM((reach, 16, capacity), F32)],
        name="pack",
    )(
        to_lanes,
        source,
        metric,
        drop_elem.reshape(reach, 1, capacity),
        drop_coord.reshape(3 * reach, 1, capacity),
        drop_vel.reshape(3 * reach, 1, capacity),
        drop_prop,
        drop_counts,
    )

    got = [
        lax.ppermute(value, "stream", neighbour_pairs(slabs, *route))
        for value, route in zip(routed, ROUTES)
    ]
    gathered = packed[None]
    bit = 1
    while bit < DEPTH:
        gathered = jnp.concatenate(
            [gathered, lax.ppermute(gathered, "stream", bit_pairs(slabs, bit))], 0
        )
        bit *= 2
    pieces = [gathered] + [
        lax.ppermute(gathered, "stream", neighbour_pairs(slabs, DEPTH, odd))
        for odd in (0, 1)
    ]
    columns = [pieces]
    bit = 1
    while bit < cols:
        columns = columns + [
            [lax.ppermute(piece, "cross", bit_pairs(cols, bit)) for piece in group]
            for group in columns
        ]
        bit *= 2
    flat = [piece for group in columns for piece in group]

    span = 2 * DEPTH - 1
    field = (cols, NODES, NODES, lanes)
    scratch_bytes = 4 * (9 * DEPTH + 1 + 5 * span) * int(np.prod(field))
    pressure, momentum, face_even, face_odd, *accels = pl.pallas_call(
        lambda *refs: main_kernel(slabs, cols, *refs),
        out_shape=[f32(NODES, NODES, lanes), near(3, NODES, NODES, lanes)]
        + [near(3, NODES, lanes)] * 2
        + [near(NODES, capacity)] * 5,
        in_specs=[vmem] * (9 + 3 * cols),
        out_specs=[vmem] * 9,
        scratch_shapes=[
            pltpu.VMEM((4 * DEPTH - 1,) + field, F32),
            pltpu.VMEM((4 * DEPTH - 1, cols, NODES, lanes), F32),
            pltpu.VMEM((span,) + field, F32),
            pltpu.VMEM((span,) + field, F32),
            pltpu.VMEM((span,) + field, F32),
            pltpu.VMEM((span + 2,) + field, F32),
            pltpu.VMEM((span + 2,) + field, F32),
        ],
        compiler_params=pltpu.CompilerParams(vmem_limit_bytes=2 * scratch_bytes + 2**23),
        name="sweeps_and_droplets",
    )(
        tiles,
        stiff_w,
        deriv_w,
        *[held(piece) for piece in flat],
        base_velocity,
        held(own),
        *[held(value) for value in got],
    )
    acc_own, acc_e1, acc_o1, acc_e2, acc_o2 = accels

    got_e2, got_o2 = [
        lax.ppermute(value, "stream", neighbour_pairs(slabs, *route))
        for value, route in zip((acc_e2, acc_o2), ROUTES[2:])
    ]
    face_even = lax.ppermute(face_even, "cross", neighbour_pairs(cols, 1, 0))
    if cols > 2:
        face_odd = lax.ppermute(face_odd, "cross", neighbour_pairs(cols, 1, 1))
    momentum, send_e1, send_o1 = pl.pallas_call(
        lambda *refs: middle_kernel(cols, *refs),
        out_shape=[near(3, NODES, NODES, lanes)] + [near(4, NODES, lanes)] * 2,
        in_specs=[vmem] * 5,
        out_specs=[vmem] * 3,
        name="cross_faces",
    )(*[held(value) for value in (momentum, face_even, face_odd, acc_e1, acc_o1)])
    got_e1, got_o1 = [
        lax.ppermute(value, "stream", neighbour_pairs(slabs, *route))
        for value, route in zip((send_e1, send_o1), ROUTES[:2])
    ]
    momentum, accel = pl.pallas_call(
        lambda *refs: last_kernel(reach, *refs),
        out_shape=[f32(3, NODES, NODES, lanes), f32(3 * reach, 1, capacity)],
        in_specs=[vmem] * 6,
        out_specs=[vmem] * 2,
        name="stream_faces",
    )(*[held(value) for value in (momentum, got_e1, got_o1, acc_own, got_e2, got_o2)])
    return (pressure, momentum, accel.reshape(1, 1, reach, 3, capacity))


def solution(mesh):
    in_specs = (
        P("stream", "cross", None),
        P("stream", "cross", None),
        P(None, "stream", "cross", None),
        P("stream", "cross", None, None),
        P("stream", "cross", None, None, None),
        P("stream", "cross", None, None, None),
        P("stream", "cross", None, None, None),
        P("stream", "cross", None),
    )
    out_specs = (
        P("stream", "cross", None),
        P(None, "stream", "cross", None),
        P("stream", "cross", None, None, None),
    )
    return jax.shard_map(step, mesh=mesh, in_specs=in_specs, out_specs=out_specs, check_vma=False)
```

profile of v0, /device:TPU:8, one launch (start us, length us, event | category | flops | bytes accessed | tf_op | source)
XLA Modules:
  0.0 54.8 jit_solution(2897315411194665470)
XLA Ops:
  0.6 0.0 copy-start.3
  0.6 1.0 %pack.1 = (f32[9,8,128]{2,1,0:T(8,128)S(1)}, f32[16,128]{1,0:T(8,128)S(1)}, f32[16,128]{1,0:T(8,128)S(1)}, f32[16,128]{1,0:T(8,128)S(1)}, f32[16,128]{1,0:T(8,128)S(1)}, /*index=5*/f32[16,128]{1,0:T(8,128)S(1)}) custom-call(f32[16,128]{1,0:T(8,128)} %constant.11.clone.refs_0_, f32[8,8,128]{2,1,0:T(8,128)} %refs_1_.2, f32[1,1,16]{2,1,0:T(1,128)} %refs_2_.2, ...), custom_call_target="tpu_custom_call" | custom-call | tf_op jit(solution)/shard_map/pack/pallas_call | solution.py:496
  1.6 1.5 %collective-permute-start = (f32[1,9,8,128]{3,2,1,0:T(8,128)S(1)}, f32[1,9,8,128]{3,2,1,0:T(8,128)S(1)}, u32[]{:S(2)}, u32[]{:S(2)}) collective-permute-start(f32[1,9,8,128]{3,2,1,0:T(8,128)S(1)} %bitcast.7), channel_id=1, source_target_pairs={{0,2},{2,0},{4,6},{6,4},{8,10},{10,8},{12,14},{14,12},{16,18},{18,... | collective-permute-start | bytes 110600 | tf_op jit(solution)/shard_map/ppermute | solution.py:522
  3.1 2.5 %collective-permute-done = f32[1,9,8,128]{3,2,1,0:T(8,128)S(1)} collective-permute-done((f32[1,9,8,128]{3,2,1,0:T(8,128)S(1)}, f32[1,9,8,128]{3,2,1,0:T(8,128)S(1)}, u32[]{:S(2)}, u32[]{:S(2)}) %collective-permute-start) | collective-permute-done | bytes 36896 | tf_op jit(solution)/shard_map/ppermute | solution.py:522
  5.6 0.0 copy-start.2
  5.6 0.0 copy-start
  5.6 0.0 copy-start.1
  5.6 1.6 %collective-permute-start.1 = (f32[2,9,8,128]{3,2,1,0:T(8,128)S(1)}, f32[2,9,8,128]{3,2,1,0:T(8,128)S(1)}, u32[]{:S(2)}, u32[]{:S(2)}) collective-permute-start(f32[2,9,8,128]{3,2,1,0:T(8,128)S(1)} %pad_maximum_fusion.1), channel_id=1, source_target_pairs={{0,4},{2,6},{4,0},{6,2},{8,12},{10,14},{12,8},{14,10},{16,20},{18,... | collective-permute-start | bytes 221192 | tf_op jit(solution)/shard_map/ppermute | solution.py:522
  7.2 2.8 %collective-permute-done.1 = f32[2,9,8,128]{3,2,1,0:T(8,128)S(1)} collective-permute-done((f32[2,9,8,128]{3,2,1,0:T(8,128)S(1)}, f32[2,9,8,128]{3,2,1,0:T(8,128)S(1)}, u32[]{:S(2)}, u32[]{:S(2)}) %collective-permute-start.1) | collective-permute-done | bytes 73760 | tf_op jit(solution)/shard_map/ppermute | solution.py:522
  10.0 3.5 %collective-permute-start.3 = (f32[4,9,8,128]{3,2,1,0:T(8,128)S(1)}, f32[4,9,8,128]{3,2,1,0:T(8,128)S(1)}, u32[]{:S(2)}, u32[]{:S(2)}) collective-permute-start(f32[4,9,8,128]{3,2,1,0:T(8,128)S(1)} %pad_maximum_fusion.refs_3_), channel_id=1, source_target_pairs={{8,16},{16,8},{10,18},{18,10},{12,20},{20,12},{14,22},{22,14},{9,1... | collective-permute-start | bytes 442376 | tf_op jit(solution)/shard_map/ppermute | solution.py:526
  13.5 0.1 collective-permute-start.2
  13.6 0.1 collective-permute-start.4
  13.7 3.4 %collective-permute-done.3.refs_5_ = f32[4,9,8,128]{3,2,1,0:T(8,128)S(1)} collective-permute-done((f32[4,9,8,128]{3,2,1,0:T(8,128)S(1)}, f32[4,9,8,128]{3,2,1,0:T(8,128)S(1)}, u32[]{:S(2)}, u32[]{:S(2)}) %collective-permute-start.3) | collective-permute-done | bytes 147488 | tf_op jit(solution)/shard_map/ppermute | solution.py:526
  17.1 0.0 collective-permute-start.6
  17.1 1.7 %collective-permute-done.2.refs_4_ = f32[4,9,8,128]{3,2,1,0:T(8,128)S(1)} collective-permute-done((f32[4,9,8,128]{3,2,1,0:T(8,128)S(1)}, f32[4,9,8,128]{3,2,1,0:T(8,128)S(1)}, u32[]{:S(2)}, u32[]{:S(2)}) %collective-permute-start.2) | collective-permute-done | bytes 147488 | tf_op jit(solution)/shard_map/ppermute | solution.py:526
  18.7 0.0 collective-permute-start.5
  18.7 1.5 %collective-permute-start.7 = (f32[16,128]{1,0:T(8,128)S(1)}, f32[16,128]{1,0:T(8,128)S(1)}, u32[]{:S(2)}, u32[]{:S(2)}) collective-permute-start(f32[16,128]{1,0:T(8,128)S(1)} %get-tuple-element.25), channel_id=1, source_target_pairs={{0,2},{2,0},{4,6},{6,4},{8,10},{10,8},{12,14},{14,12},{16,18},{18,... | collective-permute-start | bytes 24584 | tf_op jit(solution)/shard_map/ppermute | solution.py:515
  20.2 2.8 %collective-permute-start.8 = (f32[16,128]{1,0:T(8,128)S(1)}, f32[16,128]{1,0:T(8,128)S(1)}, u32[]{:S(2)}, u32[]{:S(2)}) collective-permute-start(f32[16,128]{1,0:T(8,128)S(1)} %get-tuple-element.26), channel_id=1, source_target_pairs={{2,4},{4,2},{6,8},{8,6},{10,12},{12,10},{14,16},{16,14},{18,20},{2... | collective-permute-start | bytes 24584 | tf_op jit(solution)/shard_map/ppermute | solution.py:515
  23.1 0.0 collective-permute-done.7.refs_11_
  23.1 1.1 %collective-permute-start.9 = (f32[16,128]{1,0:T(8,128)S(1)}, f32[16,128]{1,0:T(8,128)S(1)}, u32[]{:S(2)}, u32[]{:S(2)}) collective-permute-start(f32[16,128]{1,0:T(8,128)S(1)} %get-tuple-element.27), channel_id=1, source_target_pairs={{0,4},{4,0},{2,6},{6,2},{8,12},{12,8},{10,14},{14,10},{16,20},{20,... | collective-permute-start | bytes 24584 | tf_op jit(solution)/shard_map/ppermute | solution.py:515
  24.2 3.4 %collective-permute-done.8.refs_12_ = f32[16,128]{1,0:T(8,128)S(1)} collective-permute-done((f32[16,128]{1,0:T(8,128)S(1)}, f32[16,128]{1,0:T(8,128)S(1)}, u32[]{:S(2)}, u32[]{:S(2)}) %collective-permute-start.8) | collective-permute-done | bytes 8224 | tf_op jit(solution)/shard_map/ppermute | solution.py:515
  27.6 2.0 %collective-permute-start.10 = (f32[16,128]{1,0:T(8,128)S(1)}, f32[16,128]{1,0:T(8,128)S(1)}, u32[]{:S(2)}, u32[]{:S(2)}) collective-permute-start(f32[16,128]{1,0:T(8,128)S(1)} %get-tuple-element.28), channel_id=1, source_target_pairs={{4,8},{8,4},{6,10},{10,6},{12,16},{16,12},{14,18},{18,14},{20,24},... | collective-permute-start | bytes 24584 | tf_op jit(solution)/shard_map/ppermute | solution.py:515
  29.5 0.0 collective-permute-done.9.refs_13_
  29.5 4.5 %collective-permute-done.10.refs_14_ = f32[16,128]{1,0:T(8,128)S(1)} collective-permute-done((f32[16,128]{1,0:T(8,128)S(1)}, f32[16,128]{1,0:T(8,128)S(1)}, u32[]{:S(2)}, u32[]{:S(2)}) %collective-permute-start.10) | collective-permute-done | bytes 8224 | tf_op jit(solution)/shard_map/ppermute | solution.py:515
  34.0 0.0 collective-permute-done.4.refs_6_
  34.0 0.0 collective-permute-done.6.refs_8_
  34.0 0.0 collective-permute-done.5.refs_7_
  34.0 0.0 copy-done.3
  34.0 0.0 copy-done.2
  34.0 0.0 copy-done
  34.0 0.0 copy-done.1
  34.1 6.9 %sweeps_and_droplets.1 = (f32[8,8,128]{2,1,0:T(8,128)}, f32[3,8,8,128]{3,2,1,0:T(8,128)S(1)}, f32[3,8,128]{2,1,0:T(8,128)S(1)}, f32[3,8,128]{2,1,0:T(8,128)S(1)}...) custom-call(f32[32,8,128]{2,1,0:T(8,128)S(1)} %copy-done.2, ...), custom_call_target="tpu_custom_call" | custom-call | tf_op jit(solution)/shard_map/sweeps_and_droplets/pallas_call | solution.py:542
  41.0 0.0 collective-permute-start.11
  41.0 1.2 %collective-permute-done.11.refs_1_ = f32[3,8,128]{2,1,0:T(8,128)S(1)} collective-permute-done((f32[3,8,128]{2,1,0:T(8,128)S(1)}, f32[3,8,128]{2,1,0:T(8,128)S(1)}, u32[]{:S(2)}, u32[]{:S(2)}) %collective-permute-start.11) | collective-permute-done | bytes 12320 | tf_op jit(solution)/shard_map/ppermute | solution.py:575
  42.2 0.1 collective-permute-start.12
  42.3 3.4 %collective-permute-start.13 = (f32[4,8,128]{2,1,0:T(8,128)S(1)}, f32[4,8,128]{2,1,0:T(8,128)S(1)}, u32[]{:S(2)}, u32[]{:S(2)}) collective-permute-start(f32[4,8,128]{2,1,0:T(8,128)S(1)} %get-tuple-element.37), channel_id=1, source_target_pairs={{2,4},{4,2},{6,8},{8,6},{10,12},{12,10},{14,16},{16,14},{18,20},{2... | collective-permute-start | bytes 49160 | tf_op jit(solution)/shard_map/ppermute | solution.py:586
  45.7 2.0 %collective-permute-start.14 = (f32[8,128]{1,0:T(8,128)S(1)}, f32[8,128]{1,0:T(8,128)S(1)}, u32[]{:S(2)}, u32[]{:S(2)}) collective-permute-start(f32[8,128]{1,0:T(8,128)S(1)} %get-tuple-element.39), channel_id=1, source_target_pairs={{0,4},{4,0},{2,6},{6,2},{8,12},{12,8},{10,14},{14,10},{16,20},{20,... | collective-permute-start | bytes 12296 | tf_op jit(solution)/shard_map/ppermute | solution.py:572
  47.7 1.9 %collective-permute-start.15 = (f32[8,128]{1,0:T(8,128)S(1)}, f32[8,128]{1,0:T(8,128)S(1)}, u32[]{:S(2)}, u32[]{:S(2)}) collective-permute-start(f32[8,128]{1,0:T(8,128)S(1)} %get-tuple-element.40), channel_id=1, source_target_pairs={{4,8},{8,4},{6,10},{10,6},{12,16},{16,12},{14,18},{18,14},{20,24},... | collective-permute-start | bytes 12296 | tf_op jit(solution)/shard_map/ppermute | solution.py:572
  49.6 0.0 collective-permute-done.14.refs_4_
  49.7 4.5 %collective-permute-done.15.refs_5_ = f32[8,128]{1,0:T(8,128)S(1)} collective-permute-done((f32[8,128]{1,0:T(8,128)S(1)}, f32[8,128]{1,0:T(8,128)S(1)}, u32[]{:S(2)}, u32[]{:S(2)}) %collective-permute-start.15) | collective-permute-done | bytes 4128 | tf_op jit(solution)/shard_map/ppermute | solution.py:572
  54.1 0.0 collective-permute-done.12.refs_1_
  54.1 0.0 collective-permute-done.13.refs_2_
  54.1 0.7 %stream_faces.1 = (f32[3,8,8,128]{3,2,1,0:T(8,128)}, f32[15,1,128]{2,1,0:T(1,128)}) custom-call(f32[3,8,8,128]{3,2,1,0:T(8,128)S(1)} %get-tuple-element.35.refs_0_, f32[4,8,128]{2,1,0:T(8,128)S(1)} %collective-permute-done.12.refs_1_, f32[4,8,128]{2,1,0:T(8,128)S(1)} %collective-permute-done.13.refs_2_, f32[8,128]{1,0:T(8,128)S(1)} %get-tuple-element.38.refs_3_, ...), custom_call_target="tpu_custom_call" | custom-call | tf_op jit(solution)/shard_map/stream_faces/pallas_call | solution.py:589
  (3 shorter events, 0.1 us)
Async XLA Ops:
  0.6 33.4 %copy-start.3 = (f32[3,8,8,128]{3,2,1,0:T(8,128)S(1)}, f32[3,8,8,128]{3,2,1,0:T(8,128)}, u32[]{:S(2)}) copy-start(f32[3,8,8,128]{3,2,1,0:T(8,128)} %refs_9_.1) | copy-start | bytes 294916
  1.6 4.0 %collective-permute-start = (f32[1,9,8,128]{3,2,1,0:T(8,128)S(1)}, f32[1,9,8,128]{3,2,1,0:T(8,128)S(1)}, u32[]{:S(2)}, u32[]{:S(2)}) collective-permute-start(f32[1,9,8,128]{3,2,1,0:T(8,128)S(1)} %bitcast.7), channel_id=1, source_target_pairs={{0,2},{2,0},{4,6},{6,4},{8,10},{10,8},{12,14},{14,12},{16,18},{18,... | collective-permute-start | bytes 110600 | tf_op jit(solution)/shard_map/ppermute | solution.py:522
  5.6 28.5 %copy-start.2 = (f32[32,8,128]{2,1,0:T(8,128)S(1)}, f32[32,8,128]{2,1,0:T(8,128)}, u32[]{:S(2)}) copy-start(f32[32,8,128]{2,1,0:T(8,128)} %constant.8.clone.refs_0_) | copy-start | bytes 393220
  5.6 28.5 %copy-start = (bf16[256,256]{1,0:T(8,128)(2,1)S(1)}, bf16[256,256]{1,0:T(8,128)(2,1)}, u32[]{:S(2)}) copy-start(bf16[256,256]{1,0:T(8,128)(2,1)} %constant.10.clone.refs_2_) | copy-start | bytes 393220
  5.6 28.5 %copy-start.1 = (bf16[256,256]{1,0:T(8,128)(2,1)S(1)}, bf16[256,256]{1,0:T(8,128)(2,1)}, u32[]{:S(2)}) copy-start(bf16[256,256]{1,0:T(8,128)(2,1)} %constant.9.clone.refs_1_) | copy-start | bytes 393220
  5.6 4.4 %collective-permute-start.1 = (f32[2,9,8,128]{3,2,1,0:T(8,128)S(1)}, f32[2,9,8,128]{3,2,1,0:T(8,128)S(1)}, u32[]{:S(2)}, u32[]{:S(2)}) collective-permute-start(f32[2,9,8,128]{3,2,1,0:T(8,128)S(1)} %pad_maximum_fusion.1), channel_id=1, source_target_pairs={{0,4},{2,6},{4,0},{6,2},{8,12},{10,14},{12,8},{14,10},{16,20},{18,... | collective-permute-start | bytes 221192 | tf_op jit(solution)/shard_map/ppermute | solution.py:522
  10.0 7.0 %collective-permute-start.3 = (f32[4,9,8,128]{3,2,1,0:T(8,128)S(1)}, f32[4,9,8,128]{3,2,1,0:T(8,128)S(1)}, u32[]{:S(2)}, u32[]{:S(2)}) collective-permute-start(f32[4,9,8,128]{3,2,1,0:T(8,128)S(1)} %pad_maximum_fusion.refs_3_), channel_id=1, source_target_pairs={{8,16},{16,8},{10,18},{18,10},{12,20},{20,12},{14,22},{22,14},{9,1... | collective-permute-start | bytes 442376 | tf_op jit(solution)/shard_map/ppermute | solution.py:526
  13.5 5.2 %collective-permute-start.2 = (f32[4,9,8,128]{3,2,1,0:T(8,128)S(1)}, f32[4,9,8,128]{3,2,1,0:T(8,128)S(1)}, u32[]{:S(2)}, u32[]{:S(2)}) collective-permute-start(f32[4,9,8,128]{3,2,1,0:T(8,128)S(1)} %pad_maximum_fusion.refs_3_), channel_id=1, source_target_pairs={{0,8},{8,0},{2,10},{10,2},{4,12},{12,4},{6,14},{14,6},{16,24},{24,... | collective-permute-start | bytes 442376 | tf_op jit(solution)/shard_map/ppermute | solution.py:526
  13.6 20.4 %collective-permute-start.4 = (f32[4,9,8,128]{3,2,1,0:T(8,128)S(1)}, f32[4,9,8,128]{3,2,1,0:T(8,128)S(1)}, u32[]{:S(2)}, u32[]{:S(2)}) collective-permute-start(f32[4,9,8,128]{3,2,1,0:T(8,128)S(1)} %pad_maximum_fusion.refs_3_), channel_id=1, source_target_pairs={{0,1},{1,0},{2,3},{3,2},{4,5},{5,4},{6,7},{7,6},{8,9},{9,8},{10,11... | collective-permute-start | bytes 442376 | tf_op jit(solution)/shard_map/ppermute | solution.py:533
  17.1 16.9 %collective-permute-start.6 = (f32[4,9,8,128]{3,2,1,0:T(8,128)S(1)}, f32[4,9,8,128]{3,2,1,0:T(8,128)S(1)}, u32[]{:S(2)}, u32[]{:S(2)}) collective-permute-start(f32[4,9,8,128]{3,2,1,0:T(8,128)S(1)} %collective-permute-done.3.refs_5_), channel_id=1, source_target_pairs={{0,1},{1,0},{2,3},{3,2},{4,5},{5,4},{6,7},{7,6},{8,9},{9,8},{10,11... | collective-permute-start | bytes 442376 | tf_op jit(solution)/shard_map/ppermute | solution.py:533
  18.7 15.3 %collective-permute-start.5 = (f32[4,9,8,128]{3,2,1,0:T(8,128)S(1)}, f32[4,9,8,128]{3,2,1,0:T(8,128)S(1)}, u32[]{:S(2)}, u32[]{:S(2)}) collective-permute-start(f32[4,9,8,128]{3,2,1,0:T(8,128)S(1)} %collective-permute-done.2.refs_4_), channel_id=1, source_target_pairs={{0,1},{1,0},{2,3},{3,2},{4,5},{5,4},{6,7},{7,6},{8,9},{9,8},{10,11... | collective-permute-start | bytes 442376 | tf_op jit(solution)/shard_map/ppermute | solution.py:533
  18.7 4.3 %collective-permute-start.7 = (f32[16,128]{1,0:T(8,128)S(1)}, f32[16,128]{1,0:T(8,128)S(1)}, u32[]{:S(2)}, u32[]{:S(2)}) collective-permute-start(f32[16,128]{1,0:T(8,128)S(1)} %get-tuple-element.25), channel_id=1, source_target_pairs={{0,2},{2,0},{4,6},{6,4},{8,10},{10,8},{12,14},{14,12},{16,18},{18,... | collective-permute-start | bytes 24584 | tf_op jit(solution)/shard_map/ppermute | solution.py:515
  20.2 7.3 %collective-permute-start.8 = (f32[16,128]{1,0:T(8,128)S(1)}, f32[16,128]{1,0:T(8,128)S(1)}, u32[]{:S(2)}, u32[]{:S(2)}) collective-permute-start(f32[16,128]{1,0:T(8,128)S(1)} %get-tuple-element.26), channel_id=1, source_target_pairs={{2,4},{4,2},{6,8},{8,6},{10,12},{12,10},{14,16},{16,14},{18,20},{2... | collective-permute-start | bytes 24584 | tf_op jit(solution)/shard_map/ppermute | solution.py:515
  23.1 6.5 %collective-permute-start.9 = (f32[16,128]{1,0:T(8,128)S(1)}, f32[16,128]{1,0:T(8,128)S(1)}, u32[]{:S(2)}, u32[]{:S(2)}) collective-permute-start(f32[16,128]{1,0:T(8,128)S(1)} %get-tuple-element.27), channel_id=1, source_target_pairs={{0,4},{4,0},{2,6},{6,2},{8,12},{12,8},{10,14},{14,10},{16,20},{20,... | collective-permute-start | bytes 24584 | tf_op jit(solution)/shard_map/ppermute | solution.py:515
  27.6 6.4 %collective-permute-start.10 = (f32[16,128]{1,0:T(8,128)S(1)}, f32[16,128]{1,0:T(8,128)S(1)}, u32[]{:S(2)}, u32[]{:S(2)}) collective-permute-start(f32[16,128]{1,0:T(8,128)S(1)} %get-tuple-element.28), channel_id=1, source_target_pairs={{4,8},{8,4},{6,10},{10,6},{12,16},{16,12},{14,18},{18,14},{20,24},... | collective-permute-start | bytes 24584 | tf_op jit(solution)/shard_map/ppermute | solution.py:515
  41.0 1.2 %collective-permute-start.11 = (f32[3,8,128]{2,1,0:T(8,128)S(1)}, f32[3,8,128]{2,1,0:T(8,128)S(1)}, u32[]{:S(2)}, u32[]{:S(2)}) collective-permute-start(f32[3,8,128]{2,1,0:T(8,128)S(1)} %get-tuple-element.31), channel_id=1, source_target_pairs={{0,1},{1,0},{2,3},{3,2},{4,5},{5,4},{6,7},{7,6},{8,9},{9,8},{10,11... | collective-permute-start | bytes 36872 | tf_op jit(solution)/shard_map/ppermute | solution.py:575
  42.2 11.9 %collective-permute-start.12 = (f32[4,8,128]{2,1,0:T(8,128)S(1)}, f32[4,8,128]{2,1,0:T(8,128)S(1)}, u32[]{:S(2)}, u32[]{:S(2)}) collective-permute-start(f32[4,8,128]{2,1,0:T(8,128)S(1)} %get-tuple-element.36), channel_id=1, source_target_pairs={{0,2},{2,0},{4,6},{6,4},{8,10},{10,8},{12,14},{14,12},{16,18},{18,... | collective-permute-start | bytes 49160 | tf_op jit(solution)/shard_map/ppermute | solution.py:586
  42.3 11.8 %collective-permute-start.13 = (f32[4,8,128]{2,1,0:T(8,128)S(1)}, f32[4,8,128]{2,1,0:T(8,128)S(1)}, u32[]{:S(2)}, u32[]{:S(2)}) collective-permute-start(f32[4,8,128]{2,1,0:T(8,128)S(1)} %get-tuple-element.37), channel_id=1, source_target_pairs={{2,4},{4,2},{6,8},{8,6},{10,12},{12,10},{14,16},{16,14},{18,20},{2... | collective-permute-start | bytes 49160 | tf_op jit(solution)/shard_map/ppermute | solution.py:586
  45.7 3.9 %collective-permute-start.14 = (f32[8,128]{1,0:T(8,128)S(1)}, f32[8,128]{1,0:T(8,128)S(1)}, u32[]{:S(2)}, u32[]{:S(2)}) collective-permute-start(f32[8,128]{1,0:T(8,128)S(1)} %get-tuple-element.39), channel_id=1, source_target_pairs={{0,4},{4,0},{2,6},{6,2},{8,12},{12,8},{10,14},{14,10},{16,20},{20,... | collective-permute-start | bytes 12296 | tf_op jit(solution)/shard_map/ppermute | solution.py:572
  47.7 6.4 %collective-permute-start.15 = (f32[8,128]{1,0:T(8,128)S(1)}, f32[8,128]{1,0:T(8,128)S(1)}, u32[]{:S(2)}, u32[]{:S(2)}) collective-permute-start(f32[8,128]{1,0:T(8,128)S(1)} %get-tuple-element.40), channel_id=1, source_target_pairs={{4,8},{8,4},{6,10},{10,6},{12,16},{16,12},{14,18},{18,14},{20,24},... | collective-permute-start | bytes 12296 | tf_op jit(solution)/shard_map/ppermute | solution.py:572
where the time goes:
time: 55 us; the launch traced here: 54.8 us
  waiting for transfers between devices  23.8 us (43%)
  starting transfers between devices  21.5 us (39%)
  Pallas kernels  8.6 us (16%)
  between operations  0.8 us (1%)
    ppermute x8, starting transfers between devices, step(): lax.ppermute(value, 'stream', neighbour_pairs(slabs, *route))  14.8 us
    ppermute x8, waiting for transfers between devices, step(): lax.ppermute(value, 'stream', neighbour_pairs(slabs, *route))  12.3 us
    pallas_call x1, Pallas kernels, step(): pl.pallas_call(lambda *refs: main_kernel(slabs, cols, *refs), out_shape=[...  6.92 us
    ppermute x2, waiting for transfers between devices, step(): lax.ppermute(gathered, 'stream', bit_pairs(slabs, bit))  5.3 us
    ppermute x2, waiting for transfers between devices, step(): lax.ppermute(gathered, 'stream', neighbour_pairs(slabs, DEPTH, odd))  5.05 us
    ppermute x2, starting transfers between devices, step(): lax.ppermute(gathered, 'stream', neighbour_pairs(slabs, DEPTH, odd))  3.56 us
    ppermute x2, starting transfers between devices, step(): lax.ppermute(gathered, 'stream', bit_pairs(slabs, bit))  3.08 us
    ppermute x1, waiting for transfers between devices, step(): face_even = lax.ppermute(face_even, 'cross', neighbour_pairs(cols, 1, 0))  1.18 us
  transfers between devices with their start and end apart: 16, of which 8 were waited for; matrix products, arithmetic and copies ran while one was open for 0% of the time, Pallas kernels for 0%

commit v1 on v0

--- a/solution.py
+++ b/solution.py
@@ -25,7 +25,6 @@
 ]
 F32 = jnp.float32
 BF16 = jnp.bfloat16
-ROUTES = ((1, 0), (1, 1), (2, 0), (2, 1))
 
 
 def legendre_seven(points):
@@ -74,6 +73,10 @@
     ).astype(jnp.bfloat16)
 
 
+F_FACE = (DEPTH - 1) * NODES
+F_META = F_FACE + 1
+F_COUNT = F_FACE + 2
+ROUTES = ((1, 0), (1, 1), (2, 0), (2, 1))
 T_KY, T_DY = 0, 8
 T_WJ, T_QJ, T_WK, T_QK, T_Z7, T_Z0, T_Y7, T_Y0 = range(16, 24)
 T_NODE = 24
@@ -107,23 +110,59 @@
     return tiles.astype(np.float32)
 
 
-def bit_pairs(count, bit):
-    return [(i, i ^ bit) for i in range(count)]
-
-
-def neighbour_pairs(count, distance, odd):
+def swapped_bit(slabs, cols, bit):
+    return [
+        (i * cols + j, (i ^ bit) * cols + (j ^ 1)) for i in range(slabs) for j in range(cols)
+    ]
+
+
+def neighbours(slabs, cols, distance, odd, swap=0):
+    partner = {}
+    for low in range(slabs - distance):
+        if (low // distance) % 2 == odd:
+            partner[low] = low + distance
+            partner[low + distance] = low
     pairs = []
-    for low in range(count - distance):
-        if (low // distance) % 2 == odd:
-            pairs += [(low, low + distance), (low + distance, low)]
+    for i in range(slabs):
+        for j in range(cols):
+            if i in partner:
+                pairs.append((i * cols + j, partner[i] * cols + (j ^ swap)))
+            else:
+                pairs.append((i * cols + j, i * cols + (j ^ 1)))
     return pairs
 
 
-def route_block(position, route, reach):
+def column_pairs(cols, bit):
+    return [(j, j ^ bit) for j in range(cols)]
+
+
+def side_pairs(cols, odd):
+    pairs = []
+    for low in range(cols - 1):
+        if low % 2 == odd:
+            pairs += [(low, low + 1), (low + 1, low)]
+    return pairs
+
+
+def parity(slot):
+    return bin(slot).count("1") % 2
+
+
+def route_partner(position, route):
     distance, odd = route
     upward = (position // distance) % 2 == odd
+    return jnp.where(upward, position + distance, position - distance), upward
+
+
+def route_block(position, route, reach):
     middle = (reach - 1) // 2
-    return jnp.where(upward, middle + distance, middle - distance)
+    upward = route_partner(position, route)[1]
+    return jnp.where(upward, middle + route[0], middle - route[0])
+
+
+def route_open(position, route, slabs):
+    partner = route_partner(position, route)[0]
+    return jnp.logical_and(partner >= 0, partner < slabs)
 
 
 def split_value(value):
@@ -132,31 +171,49 @@
     return high, low
 
 
-def pack_kernel(cols, reach, spread_ref, source, metric, elem, coord, vel, prop, counts, *outs):
-    packed, own, routed = outs[0], outs[1], outs[2:6]
-    state = outs[6]
+def pack_kernel(cols, elem_z, source, metric, elem, coord, vel, prop, counts, first, own, *rest):
+    first[0:NODES] = source[...]
+    first[NODES] = jnp.zeros(first.shape[1:], F32)
+    first[NODES, 0:1, 0 : metric.shape[-1]] = metric[0]
+    routed, state = rest[:-1], rest[-1]
     position = lax.axis_index("stream")
     column = lax.axis_index("cross")
-    elem_z = metric.shape[-1]
-    packed[0:NODES] = source[...]
-    row = jnp.broadcast_to(metric[0, 0][None, :], (NODES, elem_z))
-    packed[NODES] = jnp.dot(row, spread_ref[...], precision=lax.Precision.HIGHEST, preferred_element_type=F32)
-    capacity = elem.shape[-1]
+    reach, _, capacity = elem.shape
     middle = (reach - 1) // 2
     slot = lax.broadcasted_iota(jnp.int32, (1, capacity), 1)
     for block in range(reach):
         base = ((position + (block - middle)) * cols + column) * elem_z
-        local = elem[block] - base + 1
         live = slot < counts[0, 0, block]
-        ids = jnp.where(live, local, 0).astype(F32)
+        ids = jnp.where(live, elem[block] - base + 1, 0).astype(F32)
         for axis in range(3):
-            state[block, axis : axis + 1, :] = coord[3 * block + axis]
-            state[block, 3 + axis : 4 + axis, :] = vel[3 * block + axis]
-        state[block, 6:8, :] = prop[0, 0, block]
-        state[block, 8:16, :] = jnp.broadcast_to(ids, (8, capacity))
+            state[block, 0, axis : axis + 1, :] = coord[3 * block + axis]
+            state[block, 0, 3 + axis : 4 + axis, :] = vel[3 * block + axis]
+        state[block, 0, 6:8, :] = prop[0, 0, block]
+        state[block, 1] = jnp.broadcast_to(ids, (NODES, capacity))
     own[...] = state[middle]
     for route, out in zip(ROUTES, routed):
         out[...] = state[route_block(position, route, reach)]
+
+
+def near_kernel(first, from_source, from_metric, out):
+    out[0] = first[...]
+    out[1, 0:NODES] = from_source[...]
+    out[1, NODES] = jnp.zeros(out.shape[2:], F32)
+    out[1, NODES, 0:1, 0 : from_metric.shape[-1]] = from_metric[0]
+
+
+def far_kernel(gathered, *outs):
+    position = lax.axis_index("stream")
+    group_even = (position // DEPTH) % 2 == 0
+    for odd, out in enumerate(outs):
+        upward = group_even if odd == 0 else jnp.logical_not(group_even)
+        for slot in range(1, DEPTH):
+            for i in range(NODES):
+                out[(slot - 1) * NODES + i] = gathered[slot, i]
+        out[F_FACE] = gathered[0, jnp.where(upward, NODES - 1, 0)]
+        out[F_META] = jnp.zeros(out.shape[1:], F32)
+        for slot in range(DEPTH):
+            out[F_META, slot : slot + 1, :] = gathered[slot, NODES, 0:1, :]
 
 
 def z_assembled(block, tiles):
@@ -216,12 +273,12 @@
 
 
 def main_kernel(slabs, cols, *refs):
-    tiles, stiff_w, deriv_w = refs[0:3]
-    pieces = refs[3 : 3 + 3 * cols]
-    base_velocity, own = refs[3 + 3 * cols : 5 + 3 * cols]
-    routed = refs[5 + 3 * cols : 9 + 3 * cols]
+    tiles, stiff_w, deriv_w, spread_w = refs[0:4]
+    pieces = refs[4 : 4 + 3 * cols]
+    base_velocity, own = refs[4 + 3 * cols : 6 + 3 * cols]
+    routed = refs[6 + 3 * cols : 10 + 3 * cols]
     (pressure, momentum, face_even, face_odd, acc_own, acc_e1, acc_o1, acc_e2, acc_o2,
-     loads, scales, resid, update, inv, work, zed) = refs[9 + 3 * cols :]
+     loads, scales, resid, update, inv, work, zed) = refs[10 + 3 * cols :]
     lanes = tiles.shape[-1]
     position = lax.axis_index("stream")
     column = lax.axis_index("cross")
@@ -231,26 +288,48 @@
     group_even = (position // DEPTH) % 2 == 0
     rank = position % DEPTH
     wjk = tiles[T_WJ] * tiles[T_WK]
-    for slot_c in range(cols):
-        col = column ^ slot_c
-        for kind in range(3):
-            if kind == 0:
-                shift = 0
-            elif kind == 1:
-                shift = jnp.where(group_even, DEPTH, -DEPTH)
-            else:
-                shift = jnp.where(group_even, -DEPTH, DEPTH)
-            piece = pieces[3 * slot_c + kind]
-            for slot in range(DEPTH):
-                at = (rank ^ slot) - rank + shift + (2 * DEPTH - 1)
-                for i in range(NODES):
-                    loads[at, col, i] = piece[slot, i] * (wjk * float(WEIGHTS[i]))
-                scales[at, col] = piece[slot, NODES]
-    wide_mid = 2 * DEPTH - 1
+    flat = (NODES, lanes)
 
     def present(offset):
         where = position + offset
         return jnp.where((where >= 0) & (where < slabs), 1.0, 0.0).astype(F32)
+
+    factors = []
+    for slot_c in range(cols):
+        near, *fars = pieces[3 * slot_c : 3 * slot_c + 3]
+        factors += [near[slot, NODES, 0:1, :] for slot in range(DEPTH)]
+        factors += [jnp.zeros((NODES - DEPTH, lanes), F32)] + [far[F_META] for far in fars]
+    high, low = split_value(jnp.concatenate(factors, 0))
+    factors = jnp.dot(
+        jnp.concatenate([high, low], 1), spread_w[...], preferred_element_type=F32
+    )
+    for slot_c in range(cols):
+        near, *fars = pieces[3 * slot_c : 3 * slot_c + 3]
+        for slot in range(DEPTH):
+            col = column ^ (slot_c ^ parity(slot))
+            at = (rank ^ slot) - rank + (2 * DEPTH - 1)
+            for i in range(NODES):
+                loads[at, col, i] = near[slot, i] * (wjk * float(WEIGHTS[i]))
+            row = 3 * NODES * slot_c + slot
+            scales[at, col] = jnp.broadcast_to(factors[row : row + 1], flat)
+        for odd, far in enumerate(fars):
+            upper = group_even if odd == 0 else jnp.logical_not(group_even)
+            shift = jnp.where(upper, DEPTH, -DEPTH)
+            inside = present(shift)
+            for slot in range(DEPTH):
+                col = column ^ (slot_c ^ parity(slot) ^ 1)
+                at = (rank ^ slot) - rank + shift + (2 * DEPTH - 1)
+                if slot > 0:
+                    for i in range(NODES):
+                        loads[at, col, i] = far[(slot - 1) * NODES + i] * (
+                            wjk * (inside * float(WEIGHTS[i]))
+                        )
+                else:
+                    layer = jnp.where(upper, 0, NODES - 1)
+                    loads[at, col, layer] = far[F_FACE] * (wjk * (inside * float(WEIGHTS[0])))
+                row = 3 * NODES * slot_c + NODES * (1 + odd) + slot
+                scales[at, col] = jnp.broadcast_to(factors[row : row + 1] * inside, flat)
+    wide_mid = 2 * DEPTH - 1
 
     def sides(offset):
         at = wide_mid + offset
@@ -376,11 +455,12 @@
         velocity.append(base_velocity[2, i] - scale * grad_z[i])
     velocity = jnp.concatenate(velocity, 0)
 
-    groups = (own,) + tuple(routed)
+    groups = [(own[0], own[1])]
+    for route, group in zip(ROUTES, routed):
+        groups.append((group[0], jnp.where(route_open(position, route, slabs), group[1], 0.0)))
     pick, bases = [], []
-    for group in groups:
+    for group, ids in groups:
         basis = [lagrange(group[axis : axis + 1, :], tiles) for axis in range(3)]
-        ids = group[8:16, :]
         pick.append(jnp.concatenate(
             [jnp.where(ids == float(e + 1), basis[2], 0.0) for e in range(lanes // NODES)], 0))
         bases.append(basis)
@@ -394,8 +474,7 @@
     )
     capacity = own.shape[-1]
     spread = []
-    for g, (group, basis) in enumerate(zip(groups, bases)):
-        ids = group[8:9, :]
+    for g, ((group, ids), basis) in enumerate(zip(groups, bases)):
         cells = [basis[1] * basis[0][i : i + 1, :] for i in range(NODES)]
         accel_rows, parts = [], []
         for comp in range(3):
@@ -405,7 +484,7 @@
                 term = partial[row : row + NODES, g * capacity : (g + 1) * capacity] * cells[i]
                 total = term if total is None else total + term
             fluid = jnp.sum(total, axis=0, keepdims=True)
-            accel = jnp.where(ids > 0.5, group[6:7, :] * (fluid - group[3 + comp : 4 + comp, :]), 0.0)
+            accel = jnp.where(ids[0:1, :] > 0.5, group[6:7, :] * (fluid - group[3 + comp : 4 + comp, :]), 0.0)
             accel_rows.append(accel)
             force = -group[7:8, :] * accel
             parts += [cells[i] * force for i in range(NODES)]
@@ -448,22 +527,23 @@
     send_o1[3] = acc_o1[...]
 
 
-def last_kernel(reach, momentum, got_e1, got_o1, acc_own, got_e2, got_o2, out, accel):
+def last_kernel(slabs, reach, momentum, got_e1, got_o1, acc_own, got_e2, got_o2, out, accel):
     position = lax.axis_index("stream")
     lower = position % 2 == 0
     top = jnp.where(lower, NODES - 1, 0)
     bottom = NODES - 1 - top
     out[...] = momentum[...]
+    opened = [route_open(position, route, slabs) for route in ROUTES]
     for comp in range(3):
-        out[comp, top] = momentum[comp, top] + got_e1[comp]
-        out[comp, bottom] = momentum[comp, bottom] + got_o1[comp]
+        out[comp, top] = momentum[comp, top] + jnp.where(opened[0], got_e1[comp], 0.0)
+        out[comp, bottom] = momentum[comp, bottom] + jnp.where(opened[1], got_o1[comp], 0.0)
     for axis in range(3):
         accel[3 * ((reach - 1) // 2) + axis] = acc_own[axis : axis + 1]
     arrived = (got_e1[3], got_o1[3], got_e2[...], got_o2[...])
-    for route, value in zip(ROUTES, arrived):
+    for route, value, there in zip(ROUTES, arrived, opened):
         block = route_block(position, route, reach)
         for axis in range(3):
-            accel[3 * block + axis] = value[axis : axis + 1]
+            accel[3 * block + axis] = jnp.where(there, value[axis : axis + 1], 0.0)
 
 
 def f32(*shape):
@@ -491,17 +571,18 @@
     tiles = jnp.asarray(table_tiles(lanes))
     stiff_w = jnp.asarray(lane_weights(STIFF, lanes))
     deriv_w = jnp.asarray(lane_weights(DERIV, lanes))
-    to_lanes = jnp.asarray(np.kron(np.eye(elem_z), np.ones((1, NODES))), F32)
-
-    packed, own, *routed = pl.pallas_call(
-        lambda *refs: pack_kernel(cols, reach, *refs),
-        out_shape=[near(NODES + 1, NODES, lanes)] + [near(16, capacity)] * 5,
-        in_specs=[vmem] * 7 + [smem],
+    to_lanes = np.zeros((lanes, lanes))
+    to_lanes[:elem_z] = np.kron(np.eye(elem_z), np.ones((1, NODES)))
+    spread_w = jnp.asarray(np.concatenate([to_lanes, to_lanes], 0), BF16)
+
+    first, own, *routed = pl.pallas_call(
+        lambda *refs: pack_kernel(cols, elem_z, *refs),
+        out_shape=[near(NODES + 1, NODES, lanes)] + [near(2, NODES, capacity)] * 5,
+        in_specs=[vmem] * 6 + [smem],
         out_specs=[vmem] * 6,
-        scratch_shapes=[pltpu.VMEM((reach, 16, capacity), F32)],
+        scratch_shapes=[pltpu.VMEM((reach, 2, NODES, capacity), F32)],
         name="pack",
     )(
-        to_lanes,
         source,
         metric,
         drop_elem.reshape(reach, 1, capacity),
@@ -510,27 +591,40 @@
         drop_prop,
         drop_counts,
     )
-
-    got = [
-        lax.ppermute(value, "stream", neighbour_pairs(slabs, *route))
+    whole = ("stream", "cross")
+
+    routed = [
+        lax.ppermute(value, whole, neighbours(slabs, cols, *route))
         for value, route in zip(routed, ROUTES)
     ]
-    gathered = packed[None]
-    bit = 1
-    while bit < DEPTH:
-        gathered = jnp.concatenate(
-            [gathered, lax.ppermute(gathered, "stream", bit_pairs(slabs, bit))], 0
-        )
-        bit *= 2
+    from_source = lax.ppermute(source, whole, swapped_bit(slabs, cols, 1))
+    from_metric = lax.ppermute(metric, whole, swapped_bit(slabs, cols, 1))
+    gathered = pl.pallas_call(
+        near_kernel,
+        out_shape=near(2, NODES + 1, NODES, lanes),
+        in_specs=[vmem] * 3,
+        out_specs=vmem,
+        name="near_pair",
+    )(held(first), held(from_source), held(from_metric))
+    gathered = jnp.concatenate(
+        [gathered, lax.ppermute(gathered, whole, swapped_bit(slabs, cols, 2))], 0
+    )
+    to_far = pl.pallas_call(
+        far_kernel,
+        out_shape=[near(F_COUNT, NODES, lanes)] * 2,
+        in_specs=[vmem],
+        out_specs=[vmem] * 2,
+        name="far_records",
+    )(held(gathered))
     pieces = [gathered] + [
-        lax.ppermute(gathered, "stream", neighbour_pairs(slabs, DEPTH, odd))
-        for odd in (0, 1)
+        lax.ppermute(value, whole, neighbours(slabs, cols, DEPTH, odd, 1))
+        for odd, value in enumerate(to_far)
     ]
     columns = [pieces]
     bit = 1
     while bit < cols:
         columns = columns + [
-            [lax.ppermute(piece, "cross", bit_pairs(cols, bit)) for piece in group]
+            [lax.ppermute(piece, "cross", column_pairs(cols, bit)) for piece in group]
             for group in columns
         ]
         bit *= 2
@@ -544,7 +638,7 @@
         out_shape=[f32(NODES, NODES, lanes), near(3, NODES, NODES, lanes)]
         + [near(3, NODES, lanes)] * 2
         + [near(NODES, capacity)] * 5,
-        in_specs=[vmem] * (9 + 3 * cols),
+        in_specs=[vmem] * (10 + 3 * cols),
         out_specs=[vmem] * 9,
         scratch_shapes=[
             pltpu.VMEM((4 * DEPTH - 1,) + field, F32),
@@ -561,20 +655,21 @@
         tiles,
         stiff_w,
         deriv_w,
+        spread_w,
         *[held(piece) for piece in flat],
         base_velocity,
         held(own),
-        *[held(value) for value in got],
+        *[held(value) for value in routed],
     )
     acc_own, acc_e1, acc_o1, acc_e2, acc_o2 = accels
 
     got_e2, got_o2 = [
-        lax.ppermute(value, "stream", neighbour_pairs(slabs, *route))
+        lax.ppermute(value, whole, neighbours(slabs, cols, *route))
         for value, route in zip((acc_e2, acc_o2), ROUTES[2:])
     ]
-    face_even = lax.ppermute(face_even, "cross", neighbour_pairs(cols, 1, 0))
+    face_even = lax.ppermute(face_even, "cross", side_pairs(cols, 0))
     if cols > 2:
-        face_odd = lax.ppermute(face_odd, "cross", neighbour_pairs(cols, 1, 1))
+        face_odd = lax.ppermute(face_odd, "cross", side_pairs(cols, 1))
     momentum, send_e1, send_o1 = pl.pallas_call(
         lambda *refs: middle_kernel(cols, *refs),
         out_shape=[near(3, NODES, NODES, lanes)] + [near(4, NODES, lanes)] * 2,
@@ -583,11 +678,11 @@
         name="cross_faces",
     )(*[held(value) for value in (momentum, face_even, face_odd, acc_e1, acc_o1)])
     got_e1, got_o1 = [
-        lax.ppermute(value, "stream", neighbour_pairs(slabs, *route))
+        lax.ppermute(value, whole, neighbours(slabs, cols, *route))
         for value, route in zip((send_e1, send_o1), ROUTES[:2])
     ]
     momentum, accel = pl.pallas_call(
-        lambda *refs: last_kernel(reach, *refs),
+        lambda *refs: last_kernel(slabs, reach, *refs),
         out_shape=[f32(3, NODES, NODES, lanes), f32(3 * reach, 1, capacity)],
         in_specs=[vmem] * 6,
         out_specs=[vmem] * 2,

time: 55 us -> 43.8 us (0.80)
  starting transfers between devices: 21.5 us -> 15.4 us
  waiting for transfers between devices: 23.8 us -> 19.3 us
    ppermute x16 -> x17, starting transfers between devices: 21.5 us -> 15.4 us  [the longest x8 7.15 us: step(): lax.ppermute(value, whole, neighbours(slabs, cols, *route))]
    ppermute x16 -> x17, waiting for transfers between devices: 23.8 us -> 19.3 us  [the longest x8 12.8 us: step(): lax.ppermute(value, whole, neighbours(slabs, cols, *route))]
    pallas_call x2 -> x4, Pallas kernels: 1.63 us -> 1.55 us  [the longest x1 0.84 us: step(): pl.pallas_call(lambda *refs: pack_kernel(cols, elem_z, *refs), out_shape=...]
  transfers between devices with their start and end apart: 16 -> 17, of which waited for: 8 -> 10; matrix products, arithmetic and copies ran while one was open for 0% -> 0% of each run, Pallas kernels for 0% -> 2%
where the time goes in v1:
time: 43.8 us; the launch traced here: 43.5 us
  waiting for transfers between devices  19.3 us (44%)
  starting transfers between devices  15.4 us (35%)
  Pallas kernels  8.06 us (18%)
  between operations  0.74 us (2%)
    ppermute x8, waiting for transfers between devices, step(): lax.ppermute(value, whole, neighbours(slabs, cols, *route))  12.8 us
    ppermute x8, starting transfers between devices, step(): lax.ppermute(value, whole, neighbours(slabs, cols, *route))  7.15 us
    pallas_call x1, Pallas kernels, step(): pl.pallas_call(lambda *refs: main_kernel(slabs, cols, *refs), out_shape=[...  6.46 us
    ppermute x2, starting transfers between devices, step(): lax.ppermute(value, whole, neighbours(slabs, cols, DEPTH, odd, 1))  2.94 us
    ppermute x1, waiting for transfers between devices, step(): lax.ppermute(gathered, whole, swapped_bit(slabs, cols, 2))  2.04 us
    ppermute x1, starting transfers between devices, step(): lax.ppermute(gathered, whole, swapped_bit(slabs, cols, 2))  1.87 us
    ppermute x2, waiting for transfers between devices, step(): lax.ppermute(value, whole, neighbours(slabs, cols, DEPTH, odd, 1))  1.78 us
    ppermute x3, starting transfers between devices, step(): lax.ppermute(piece, 'cross', column_pairs(cols, bit))  1.57 us
  transfers between devices with their start and end apart: 17, of which 10 were waited for; matrix products, arithmetic and copies ran while one was open for 0% of the time, Pallas kernels for 2%

profile of v1, /device:TPU:8, one launch (start us, length us, event | category | flops | bytes accessed | tf_op | source)
XLA Modules:
  0.0 43.5 jit_solution(2624601134905516328)
XLA Ops:
  0.6 1.0 %collective-permute-start = (f32[8,8,128]{2,1,0:T(8,128)}, f32[8,8,128]{2,1,0:T(8,128)S(1)}, u32[]{:S(2)}, u32[]{:S(2)}) collective-permute-start(f32[8,8,128]{2,1,0:T(8,128)} %refs_0_.2), channel_id=1, source_target_pairs={{0,3},{1,2},{2,1},{3,0},{4,7},{5,6},{6,5},{7,4},{8,11},{9,10},{10,... | collective-permute-start | bytes 98312 | tf_op jit(solution)/shard_map/ppermute | solution.py:600
  1.6 0.8 %collective-permute-start.1 = (f32[1,1,16]{2,1,0:T(1,128)}, f32[1,1,16]{2,1,0:T(1,128)S(1)}, u32[]{:S(2)}, u32[]{:S(2)}) collective-permute-start(f32[1,1,16]{2,1,0:T(1,128)} %refs_1_.2), channel_id=1, source_target_pairs={{0,3},{1,2},{2,1},{3,0},{4,7},{5,6},{6,5},{7,4},{8,11},{9,10},{10,... | collective-permute-start | bytes 200 | tf_op jit(solution)/shard_map/ppermute | solution.py:601
  2.4 0.8 %pack.1 = (f32[9,8,128]{2,1,0:T(8,128)S(1)}, f32[2,8,128]{2,1,0:T(8,128)S(1)}, f32[2,8,128]{2,1,0:T(8,128)S(1)}, f32[2,8,128]{2,1,0:T(8,128)S(1)}, f32[2,8,128]{2,1,0:T(8,128)S(1)}, /*index=5*/f32[2,8,128]{2,1,0:T(8,128)S(1)}) custom-call(f32[8,8,128]{2,1,0:T(8,128)} %refs_0_.2, f32[1,1,16]{2,1,0:T(1,128)} %refs_1_.2, s32[5,1,128]{2,1,0:T(1,128)} %bitcast.8, ...), custom_call_target="tpu_custom_call" | custom-call | tf_op jit(solution)/shard_map/pack/pallas_call | solution.py:578
  3.3 1.5 %collective-permute-done.1.from_metric = f32[1,1,16]{2,1,0:T(1,128)S(1)} collective-permute-done((f32[1,1,16]{2,1,0:T(1,128)}, f32[1,1,16]{2,1,0:T(1,128)S(1)}, u32[]{:S(2)}, u32[]{:S(2)}) %collective-permute-start.1) | collective-permute-done | bytes 96 | tf_op jit(solution)/shard_map/ppermute | solution.py:601
  4.8 0.0 collective-permute-done.from_source
  4.8 0.0 copy-start.3
  4.8 0.0 copy-start.4
  4.8 1.9 %collective-permute-start.2 = (f32[2,9,8,128]{3,2,1,0:T(8,128)S(1)}, f32[2,9,8,128]{3,2,1,0:T(8,128)S(1)}, u32[]{:S(2)}, u32[]{:S(2)}) collective-permute-start(f32[2,9,8,128]{3,2,1,0:T(8,128)S(1)} %near_pair.1), channel_id=1, source_target_pairs={{0,5},{1,4},{2,7},{3,6},{4,1},{5,0},{6,3},{7,2},{8,13},{9,12},{10,... | collective-permute-start | bytes 221192 | tf_op jit(solution)/shard_map/ppermute | solution.py:610
  6.6 2.0 %collective-permute-done.2 = f32[2,9,8,128]{3,2,1,0:T(8,128)S(1)} collective-permute-done((f32[2,9,8,128]{3,2,1,0:T(8,128)S(1)}, f32[2,9,8,128]{3,2,1,0:T(8,128)S(1)}, u32[]{:S(2)}, u32[]{:S(2)}) %collective-permute-start.2) | collective-permute-done | bytes 73760 | tf_op jit(solution)/shard_map/ppermute | solution.py:610
  8.7 0.0 copy-start.1
  8.7 0.0 copy-start.2
  8.7 0.0 copy-start
  8.7 0.7 %collective-permute-start.3 = (f32[26,8,128]{2,1,0:T(8,128)S(1)}, f32[26,8,128]{2,1,0:T(8,128)S(1)}, u32[]{:S(2)}, u32[]{:S(2)}) collective-permute-start(f32[26,8,128]{2,1,0:T(8,128)S(1)} %get-tuple-element.26), channel_id=1, source_target_pairs={{0,9},{1,8},{2,11},{3,10},{4,13},{5,12},{6,15},{7,14},{8,1},{9,0},... | collective-permute-start | bytes 319496 | tf_op jit(solution)/shard_map/ppermute | solution.py:620
  9.5 2.2 %collective-permute-start.4 = (f32[26,8,128]{2,1,0:T(8,128)S(1)}, f32[26,8,128]{2,1,0:T(8,128)S(1)}, u32[]{:S(2)}, u32[]{:S(2)}) collective-permute-start(f32[26,8,128]{2,1,0:T(8,128)S(1)} %get-tuple-element.27), channel_id=1, source_target_pairs={{0,1},{1,0},{2,3},{3,2},{4,5},{5,4},{6,7},{7,6},{8,17},{9,16},{10,... | collective-permute-start | bytes 319496 | tf_op jit(solution)/shard_map/ppermute | solution.py:620
  11.7 0.6 %collective-permute-start.5 = (f32[4,9,8,128]{3,2,1,0:T(8,128)S(1)}, f32[4,9,8,128]{3,2,1,0:T(8,128)S(1)}, u32[]{:S(2)}, u32[]{:S(2)}) collective-permute-start(f32[4,9,8,128]{3,2,1,0:T(8,128)S(1)} %pad_maximum_fusion.gathered.refs_4_), channel_id=1, source_target_pairs={{0,1},{1,0},{2,3},{3,2},{4,5},{5,4},{6,7},{7,6},{8,9},{9,8},{10,11... | collective-permute-start | bytes 442376 | tf_op jit(solution)/shard_map/ppermute | solution.py:627
  12.3 1.0 %collective-permute-done.3.refs_5_ = f32[26,8,128]{2,1,0:T(8,128)S(1)} collective-permute-done((f32[26,8,128]{2,1,0:T(8,128)S(1)}, f32[26,8,128]{2,1,0:T(8,128)S(1)}, u32[]{:S(2)}, u32[]{:S(2)}) %collective-permute-start.3) | collective-permute-done | bytes 106528 | tf_op jit(solution)/shard_map/ppermute | solution.py:620
  13.3 0.9 %collective-permute-start.6 = (f32[26,8,128]{2,1,0:T(8,128)S(1)}, f32[26,8,128]{2,1,0:T(8,128)S(1)}, u32[]{:S(2)}, u32[]{:S(2)}) collective-permute-start(f32[26,8,128]{2,1,0:T(8,128)S(1)} %collective-permute-done.3.refs_5_), channel_id=1, source_target_pairs={{0,1},{1,0},{2,3},{3,2},{4,5},{5,4},{6,7},{7,6},{8,9},{9,8},{10,11... | collective-permute-start | bytes 319496 | tf_op jit(solution)/shard_map/ppermute | solution.py:627
  14.2 0.8 %collective-permute-done.4.refs_6_ = f32[26,8,128]{2,1,0:T(8,128)S(1)} collective-permute-done((f32[26,8,128]{2,1,0:T(8,128)S(1)}, f32[26,8,128]{2,1,0:T(8,128)S(1)}, u32[]{:S(2)}, u32[]{:S(2)}) %collective-permute-start.4) | collective-permute-done | bytes 106528 | tf_op jit(solution)/shard_map/ppermute | solution.py:620
  15.0 0.0 collective-permute-start.7
  15.0 1.9 %collective-permute-start.8 = (f32[2,8,128]{2,1,0:T(8,128)S(1)}, f32[2,8,128]{2,1,0:T(8,128)S(1)}, u32[]{:S(2)}, u32[]{:S(2)}) collective-permute-start(f32[2,8,128]{2,1,0:T(8,128)S(1)} %get-tuple-element.29), channel_id=1, source_target_pairs={{0,2},{1,3},{2,0},{3,1},{4,6},{5,7},{6,4},{7,5},{8,10},{9,11},{10,... | collective-permute-start | bytes 24584 | tf_op jit(solution)/shard_map/ppermute | solution.py:597
  17.0 0.1 collective-permute-start.9
  17.1 1.6 %collective-permute-done.8.refs_12_ = f32[2,8,128]{2,1,0:T(8,128)S(1)} collective-permute-done((f32[2,8,128]{2,1,0:T(8,128)S(1)}, f32[2,8,128]{2,1,0:T(8,128)S(1)}, u32[]{:S(2)}, u32[]{:S(2)}) %collective-permute-start.8) | collective-permute-done | bytes 8224 | tf_op jit(solution)/shard_map/ppermute | solution.py:597
  18.7 1.6 %collective-permute-start.10 = (f32[2,8,128]{2,1,0:T(8,128)S(1)}, f32[2,8,128]{2,1,0:T(8,128)S(1)}, u32[]{:S(2)}, u32[]{:S(2)}) collective-permute-start(f32[2,8,128]{2,1,0:T(8,128)S(1)} %get-tuple-element.31), channel_id=1, source_target_pairs={{0,4},{1,5},{2,6},{3,7},{4,0},{5,1},{6,2},{7,3},{8,12},{9,13},{10,... | collective-permute-start | bytes 24584 | tf_op jit(solution)/shard_map/ppermute | solution.py:597
  20.2 2.2 %collective-permute-done.9.refs_13_ = f32[2,8,128]{2,1,0:T(8,128)S(1)} collective-permute-done((f32[2,8,128]{2,1,0:T(8,128)S(1)}, f32[2,8,128]{2,1,0:T(8,128)S(1)}, u32[]{:S(2)}, u32[]{:S(2)}) %collective-permute-start.9) | collective-permute-done | bytes 8224 | tf_op jit(solution)/shard_map/ppermute | solution.py:597
  22.4 0.0 collective-permute-start.11
  22.4 0.0 collective-permute-done.10.refs_14_
  22.4 4.5 %collective-permute-done.11.refs_15_ = f32[2,8,128]{2,1,0:T(8,128)S(1)} collective-permute-done((f32[2,8,128]{2,1,0:T(8,128)S(1)}, f32[2,8,128]{2,1,0:T(8,128)S(1)}, u32[]{:S(2)}, u32[]{:S(2)}) %collective-permute-start.11) | collective-permute-done | bytes 8224 | tf_op jit(solution)/shard_map/ppermute | solution.py:597
  27.0 0.0 collective-permute-done.5.refs_7_
  27.0 0.0 collective-permute-done.6.refs_8_
  27.0 0.0 collective-permute-done.7.refs_9_
  27.0 0.0 copy-done.3
  27.0 0.0 copy-done.4
  27.0 0.0 copy-done.1
  27.0 0.0 copy-done.2
  27.0 0.0 copy-done
  27.0 6.5 %sweeps_and_droplets.1 = (f32[8,8,128]{2,1,0:T(8,128)}, f32[3,8,8,128]{3,2,1,0:T(8,128)S(1)}, f32[3,8,128]{2,1,0:T(8,128)S(1)}, f32[3,8,128]{2,1,0:T(8,128)S(1)}...) custom-call(f32[32,8,128]{2,1,0:T(8,128)S(1)} %copy-done.2, ...), custom_call_target="tpu_custom_call" | custom-call | tf_op jit(solution)/shard_map/sweeps_and_droplets/pallas_call | solution.py:636
  33.5 0.0 collective-permute-start.12
  33.5 1.2 %collective-permute-done.12.refs_1_ = f32[3,8,128]{2,1,0:T(8,128)S(1)} collective-permute-done((f32[3,8,128]{2,1,0:T(8,128)S(1)}, f32[3,8,128]{2,1,0:T(8,128)S(1)}, u32[]{:S(2)}, u32[]{:S(2)}) %collective-permute-start.12) | collective-permute-done | bytes 12320 | tf_op jit(solution)/shard_map/ppermute | solution.py:670
  34.7 0.1 collective-permute-start.13
  34.8 1.5 %collective-permute-start.14 = (f32[4,8,128]{2,1,0:T(8,128)S(1)}, f32[4,8,128]{2,1,0:T(8,128)S(1)}, u32[]{:S(2)}, u32[]{:S(2)}) collective-permute-start(f32[4,8,128]{2,1,0:T(8,128)S(1)} %get-tuple-element.41), channel_id=1, source_target_pairs={{0,1},{1,0},{2,4},{3,5},{4,2},{5,3},{6,8},{7,9},{8,6},{9,7},{10,12... | collective-permute-start | bytes 49160 | tf_op jit(solution)/shard_map/ppermute | solution.py:681
  36.3 2.0 %collective-permute-start.15 = (f32[8,128]{1,0:T(8,128)S(1)}, f32[8,128]{1,0:T(8,128)S(1)}, u32[]{:S(2)}, u32[]{:S(2)}) collective-permute-start(f32[8,128]{1,0:T(8,128)S(1)} %get-tuple-element.43), channel_id=1, source_target_pairs={{0,4},{1,5},{2,6},{3,7},{4,0},{5,1},{6,2},{7,3},{8,12},{9,13},{10,... | collective-permute-start | bytes 12296 | tf_op jit(solution)/shard_map/ppermute | solution.py:667
  38.3 0.0 collective-permute-start.16
  38.3 1.6 %collective-permute-done.15.refs_4_ = f32[8,128]{1,0:T(8,128)S(1)} collective-permute-done((f32[8,128]{1,0:T(8,128)S(1)}, f32[8,128]{1,0:T(8,128)S(1)}, u32[]{:S(2)}, u32[]{:S(2)}) %collective-permute-start.15) | collective-permute-done | bytes 4128 | tf_op jit(solution)/shard_map/ppermute | solution.py:667
  39.9 2.9 %collective-permute-done.16.refs_5_ = f32[8,128]{1,0:T(8,128)S(1)} collective-permute-done((f32[8,128]{1,0:T(8,128)S(1)}, f32[8,128]{1,0:T(8,128)S(1)}, u32[]{:S(2)}, u32[]{:S(2)}) %collective-permute-start.16) | collective-permute-done | bytes 4128 | tf_op jit(solution)/shard_map/ppermute | solution.py:667
  42.8 0.0 collective-permute-done.13.refs_1_
  42.8 0.0 collective-permute-done.14.refs_2_
  42.8 0.7 %stream_faces.1 = (f32[3,8,8,128]{3,2,1,0:T(8,128)}, f32[15,1,128]{2,1,0:T(1,128)}) custom-call(f32[3,8,8,128]{3,2,1,0:T(8,128)S(1)} %get-tuple-element.39.refs_0_, f32[4,8,128]{2,1,0:T(8,128)S(1)} %collective-permute-done.13.refs_1_, f32[4,8,128]{2,1,0:T(8,128)S(1)} %collective-permute-done.14.refs_2_, f32[8,128]{1,0:T(8,128)S(1)} %get-tuple-element.42.refs_3_, ...), custom_call_target="tpu_custom_call" | custom-call | tf_op jit(solution)/shard_map/stream_faces/pallas_call | solution.py:684
  (4 shorter events, 0.1 us)
Async XLA Ops:
  0.6 4.1 %collective-permute-start = (f32[8,8,128]{2,1,0:T(8,128)}, f32[8,8,128]{2,1,0:T(8,128)S(1)}, u32[]{:S(2)}, u32[]{:S(2)}) collective-permute-start(f32[8,8,128]{2,1,0:T(8,128)} %refs_0_.2), channel_id=1, source_target_pairs={{0,3},{1,2},{2,1},{3,0},{4,7},{5,6},{6,5},{7,4},{8,11},{9,10},{10,... | collective-permute-start | bytes 98312 | tf_op jit(solution)/shard_map/ppermute | solution.py:600
  1.6 3.1 %collective-permute-start.1 = (f32[1,1,16]{2,1,0:T(1,128)}, f32[1,1,16]{2,1,0:T(1,128)S(1)}, u32[]{:S(2)}, u32[]{:S(2)}) collective-permute-start(f32[1,1,16]{2,1,0:T(1,128)} %refs_1_.2), channel_id=1, source_target_pairs={{0,3},{1,2},{2,1},{3,0},{4,7},{5,6},{6,5},{7,4},{8,11},{9,10},{10,... | collective-permute-start | bytes 200 | tf_op jit(solution)/shard_map/ppermute | solution.py:601
  4.8 22.2 %copy-start.3 = (f32[3,8,8,128]{3,2,1,0:T(8,128)S(1)}, f32[3,8,8,128]{3,2,1,0:T(8,128)}, u32[]{:S(2)}) copy-start(f32[3,8,8,128]{3,2,1,0:T(8,128)} %refs_10_.1) | copy-start | bytes 294916
  4.8 22.2 %copy-start.4 = (bf16[256,128]{1,0:T(8,128)(2,1)S(1)}, bf16[256,128]{1,0:T(8,128)(2,1)}, u32[]{:S(2)}) copy-start(bf16[256,128]{1,0:T(8,128)(2,1)} %constant.11.clone.refs_3_) | copy-start | bytes 196612
  4.8 3.9 %collective-permute-start.2 = (f32[2,9,8,128]{3,2,1,0:T(8,128)S(1)}, f32[2,9,8,128]{3,2,1,0:T(8,128)S(1)}, u32[]{:S(2)}, u32[]{:S(2)}) collective-permute-start(f32[2,9,8,128]{3,2,1,0:T(8,128)S(1)} %near_pair.1), channel_id=1, source_target_pairs={{0,5},{1,4},{2,7},{3,6},{4,1},{5,0},{6,3},{7,2},{8,13},{9,12},{10,... | collective-permute-start | bytes 221192 | tf_op jit(solution)/shard_map/ppermute | solution.py:610
  8.7 18.3 %copy-start.1 = (bf16[256,256]{1,0:T(8,128)(2,1)S(1)}, bf16[256,256]{1,0:T(8,128)(2,1)}, u32[]{:S(2)}) copy-start(bf16[256,256]{1,0:T(8,128)(2,1)} %constant.9.clone.refs_1_) | copy-start | bytes 393220
  8.7 18.3 %copy-start.2 = (f32[32,8,128]{2,1,0:T(8,128)S(1)}, f32[32,8,128]{2,1,0:T(8,128)}, u32[]{:S(2)}) copy-start(f32[32,8,128]{2,1,0:T(8,128)} %constant.8.clone.refs_0_) | copy-start | bytes 393220
  8.7 18.3 %copy-start = (bf16[256,256]{1,0:T(8,128)(2,1)S(1)}, bf16[256,256]{1,0:T(8,128)(2,1)}, u32[]{:S(2)}) copy-start(bf16[256,256]{1,0:T(8,128)(2,1)} %constant.10.clone.refs_2_) | copy-start | bytes 393220
  8.7 4.5 %collective-permute-start.3 = (f32[26,8,128]{2,1,0:T(8,128)S(1)}, f32[26,8,128]{2,1,0:T(8,128)S(1)}, u32[]{:S(2)}, u32[]{:S(2)}) collective-permute-start(f32[26,8,128]{2,1,0:T(8,128)S(1)} %get-tuple-element.26), channel_id=1, source_target_pairs={{0,9},{1,8},{2,11},{3,10},{4,13},{5,12},{6,15},{7,14},{8,1},{9,0},... | collective-permute-start | bytes 319496 | tf_op jit(solution)/shard_map/ppermute | solution.py:620
  9.5 5.5 %collective-permute-start.4 = (f32[26,8,128]{2,1,0:T(8,128)S(1)}, f32[26,8,128]{2,1,0:T(8,128)S(1)}, u32[]{:S(2)}, u32[]{:S(2)}) collective-permute-start(f32[26,8,128]{2,1,0:T(8,128)S(1)} %get-tuple-element.27), channel_id=1, source_target_pairs={{0,1},{1,0},{2,3},{3,2},{4,5},{5,4},{6,7},{7,6},{8,17},{9,16},{10,... | collective-permute-start | bytes 319496 | tf_op jit(solution)/shard_map/ppermute | solution.py:620
  11.7 15.3 %collective-permute-start.5 = (f32[4,9,8,128]{3,2,1,0:T(8,128)S(1)}, f32[4,9,8,128]{3,2,1,0:T(8,128)S(1)}, u32[]{:S(2)}, u32[]{:S(2)}) collective-permute-start(f32[4,9,8,128]{3,2,1,0:T(8,128)S(1)} %pad_maximum_fusion.gathered.refs_4_), channel_id=1, source_target_pairs={{0,1},{1,0},{2,3},{3,2},{4,5},{5,4},{6,7},{7,6},{8,9},{9,8},{10,11... | collective-permute-start | bytes 442376 | tf_op jit(solution)/shard_map/ppermute | solution.py:627
  13.3 13.7 %collective-permute-start.6 = (f32[26,8,128]{2,1,0:T(8,128)S(1)}, f32[26,8,128]{2,1,0:T(8,128)S(1)}, u32[]{:S(2)}, u32[]{:S(2)}) collective-permute-start(f32[26,8,128]{2,1,0:T(8,128)S(1)} %collective-permute-done.3.refs_5_), channel_id=1, source_target_pairs={{0,1},{1,0},{2,3},{3,2},{4,5},{5,4},{6,7},{7,6},{8,9},{9,8},{10,11... | collective-permute-start | bytes 319496 | tf_op jit(solution)/shard_map/ppermute | solution.py:627
  15.0 12.0 %collective-permute-start.7 = (f32[26,8,128]{2,1,0:T(8,128)S(1)}, f32[26,8,128]{2,1,0:T(8,128)S(1)}, u32[]{:S(2)}, u32[]{:S(2)}) collective-permute-start(f32[26,8,128]{2,1,0:T(8,128)S(1)} %collective-permute-done.4.refs_6_), channel_id=1, source_target_pairs={{0,1},{1,0},{2,3},{3,2},{4,5},{5,4},{6,7},{7,6},{8,9},{9,8},{10,11... | collective-permute-start | bytes 319496 | tf_op jit(solution)/shard_map/ppermute | solution.py:627
  15.0 3.7 %collective-permute-start.8 = (f32[2,8,128]{2,1,0:T(8,128)S(1)}, f32[2,8,128]{2,1,0:T(8,128)S(1)}, u32[]{:S(2)}, u32[]{:S(2)}) collective-permute-start(f32[2,8,128]{2,1,0:T(8,128)S(1)} %get-tuple-element.29), channel_id=1, source_target_pairs={{0,2},{1,3},{2,0},{3,1},{4,6},{5,7},{6,4},{7,5},{8,10},{9,11},{10,... | collective-permute-start | bytes 24584 | tf_op jit(solution)/shard_map/ppermute | solution.py:597
  17.0 5.5 %collective-permute-start.9 = (f32[2,8,128]{2,1,0:T(8,128)S(1)}, f32[2,8,128]{2,1,0:T(8,128)S(1)}, u32[]{:S(2)}, u32[]{:S(2)}) collective-permute-start(f32[2,8,128]{2,1,0:T(8,128)S(1)} %get-tuple-element.30), channel_id=1, source_target_pairs={{0,1},{1,0},{2,4},{3,5},{4,2},{5,3},{6,8},{7,9},{8,6},{9,7},{10,12... | collective-permute-start | bytes 24584 | tf_op jit(solution)/shard_map/ppermute | solution.py:597
  18.7 3.7 %collective-permute-start.10 = (f32[2,8,128]{2,1,0:T(8,128)S(1)}, f32[2,8,128]{2,1,0:T(8,128)S(1)}, u32[]{:S(2)}, u32[]{:S(2)}) collective-permute-start(f32[2,8,128]{2,1,0:T(8,128)S(1)} %get-tuple-element.31), channel_id=1, source_target_pairs={{0,4},{1,5},{2,6},{3,7},{4,0},{5,1},{6,2},{7,3},{8,12},{9,13},{10,... | collective-permute-start | bytes 24584 | tf_op jit(solution)/shard_map/ppermute | solution.py:597
  22.4 4.5 %collective-permute-start.11 = (f32[2,8,128]{2,1,0:T(8,128)S(1)}, f32[2,8,128]{2,1,0:T(8,128)S(1)}, u32[]{:S(2)}, u32[]{:S(2)}) collective-permute-start(f32[2,8,128]{2,1,0:T(8,128)S(1)} %get-tuple-element.32), channel_id=1, source_target_pairs={{0,1},{1,0},{2,3},{3,2},{4,8},{5,9},{6,10},{7,11},{8,4},{9,5},{10,... | collective-permute-start | bytes 24584 | tf_op jit(solution)/shard_map/ppermute | solution.py:597
  33.5 1.2 %collective-permute-start.12 = (f32[3,8,128]{2,1,0:T(8,128)S(1)}, f32[3,8,128]{2,1,0:T(8,128)S(1)}, u32[]{:S(2)}, u32[]{:S(2)}) collective-permute-start(f32[3,8,128]{2,1,0:T(8,128)S(1)} %get-tuple-element.35), channel_id=1, source_target_pairs={{0,1},{1,0},{2,3},{3,2},{4,5},{5,4},{6,7},{7,6},{8,9},{9,8},{10,11... | collective-permute-start | bytes 36872 | tf_op jit(solution)/shard_map/ppermute | solution.py:670
  34.7 8.1 %collective-permute-start.13 = (f32[4,8,128]{2,1,0:T(8,128)S(1)}, f32[4,8,128]{2,1,0:T(8,128)S(1)}, u32[]{:S(2)}, u32[]{:S(2)}) collective-permute-start(f32[4,8,128]{2,1,0:T(8,128)S(1)} %get-tuple-element.40), channel_id=1, source_target_pairs={{0,2},{1,3},{2,0},{3,1},{4,6},{5,7},{6,4},{7,5},{8,10},{9,11},{10,... | collective-permute-start | bytes 49160 | tf_op jit(solution)/shard_map/ppermute | solution.py:681
  34.8 8.0 %collective-permute-start.14 = (f32[4,8,128]{2,1,0:T(8,128)S(1)}, f32[4,8,128]{2,1,0:T(8,128)S(1)}, u32[]{:S(2)}, u32[]{:S(2)}) collective-permute-start(f32[4,8,128]{2,1,0:T(8,128)S(1)} %get-tuple-element.41), channel_id=1, source_target_pairs={{0,1},{1,0},{2,4},{3,5},{4,2},{5,3},{6,8},{7,9},{8,6},{9,7},{10,12... | collective-permute-start | bytes 49160 | tf_op jit(solution)/shard_map/ppermute | solution.py:681
  36.3 3.6 %collective-permute-start.15 = (f32[8,128]{1,0:T(8,128)S(1)}, f32[8,128]{1,0:T(8,128)S(1)}, u32[]{:S(2)}, u32[]{:S(2)}) collective-permute-start(f32[8,128]{1,0:T(8,128)S(1)} %get-tuple-element.43), channel_id=1, source_target_pairs={{0,4},{1,5},{2,6},{3,7},{4,0},{5,1},{6,2},{7,3},{8,12},{9,13},{10,... | collective-permute-start | bytes 12296 | tf_op jit(solution)/shard_map/ppermute | solution.py:667
  38.3 4.5 %collective-permute-start.16 = (f32[8,128]{1,0:T(8,128)S(1)}, f32[8,128]{1,0:T(8,128)S(1)}, u32[]{:S(2)}, u32[]{:S(2)}) collective-permute-start(f32[8,128]{1,0:T(8,128)S(1)} %get-tuple-element.44), channel_id=1, source_target_pairs={{0,1},{1,0},{2,3},{3,2},{4,8},{5,9},{6,10},{7,11},{8,4},{9,5},{10,... | collective-permute-start | bytes 12296 | tf_op jit(solution)/shard_map/ppermute | solution.py:667
